TPU v7x, 32 devices: a whole 2x2x4 slice. The times are simulated.
32 devices in a mesh: dp: 8 (over z, x), tensor: 4 (over y, core).
Axes of the slice: x: 2, y: 2, z: 4, core: 2. Of those that a mesh axis runs over, the one named last changes fastest.
Arguments:
- tokens: bfloat16 [16384, 768], P(('dp', 'tensor')), may hold values from -6 to 6
- input_gain: float32 [768], replicated, may hold values from 0.5 to 1.5
- input_bias: float32 [768], replicated, may hold values from -1.5 to 1.5
- post_gain: float32 [768], replicated, may hold values from 0.5 to 1.5
- post_bias: float32 [768], replicated, may hold values from -1.5 to 1.5
- query_key_value: bfloat16 [3, 768, 768], P(None, None, 'tensor'), may hold values from -0.21875 to 0.21875
- query_key_value_bias: float32 [3, 768], P(None, 'tensor'), may hold values from -1.5 to 1.5
- dense_weight: bfloat16 [768, 768], P('tensor'), may hold values from -3 to 3
- dense_bias: float32 [768], replicated, may hold values from -1.5 to 1.5
- expand_weight: bfloat16 [768, 3072], P(None, 'tensor'), may hold values from -0.21875 to 0.21875
- expand_bias: float32 [3072], P('tensor'), may hold values from -2.5 to 2.5
- contract_weight: bfloat16 [3072, 768], P('tensor'), may hold values from -0.109375 to 0.109375
- contract_bias: float32 [768], replicated, may hold values from -1.5 to 1.5
- lengths: int32 [8], P('dp'), may hold values from 102 to 2048, as said below
- cotangent: bfloat16 [16384, 768], P(('dp', 'tensor')), may hold values from -6 to 6
Outputs:
- mixed: bfloat16 [16384, 768], P(('dp', 'tensor'))
- grad_tokens: float32 [16384, 768], P(('dp', 'tensor'))
- grad_input_gain: float32 [768], replicated
- grad_input_bias: float32 [768], replicated
- grad_post_gain: float32 [768], replicated
- grad_post_bias: float32 [768], replicated
- grad_query_key_value: float32 [3, 768, 768], P(None, None, 'tensor')
- grad_query_key_value_bias: float32 [3, 768], P(None, 'tensor')
- grad_dense_weight: float32 [768, 768], P('tensor')
- grad_dense_bias: float32 [768], replicated
- grad_expand_weight: float32 [768, 3072], P(None, 'tensor')
- grad_expand_bias: float32 [3072], P('tensor')
- grad_contract_weight: float32 [3072, 768], P('tensor')
- grad_contract_bias: float32 [768], replicated
Inputs may be any that keep to these rules, and one draw needn't show every extreme that they name: lengths[s] is the number of real tokens of sentence s, the rest of its 2048 slots being padding; in every draw some sentence fills all 2048 slots.
All inputs are finite; a program needn't handle non-finite values.
Results may differ from a plain program's by a relative error of at most 0.012.
Values may be sent and summed in bfloat16 or wider, within the bound.
A program may use at most 128 MiB of HBM per device.

v0:
```python
import jax
import jax.numpy as jnp
from jax import lax
from jax.sharding import PartitionSpec as P

HD = 64
ROT = 16
LEN = 2048


EPS = 1e-05
MASKED = -1e30


def normalize(rows, gain, bias):
    values = rows.astype(jnp.float32)
    centred = values - jnp.mean(values, -1, keepdims=True)
    inverse = lax.rsqrt(jnp.mean(centred * centred, -1, keepdims=True) + EPS)
    unit = centred * inverse
    return ((unit * gain + bias).astype(jnp.bfloat16), unit, inverse)


def norm_back(grad, unit, inverse, gain):
    scaled = grad * gain
    return inverse * (
        scaled
        - jnp.mean(scaled, -1, keepdims=True)
        - unit * jnp.mean(scaled * unit, -1, keepdims=True)
    )


def angles(count):
    half = ROT // 2
    freqs = 10000.0 ** (-2.0 * jnp.arange(half, dtype=jnp.float32) / ROT)
    place = (jnp.arange(count) % LEN).astype(jnp.float32)
    angle = place[:, None] * freqs[None, :]
    return (jnp.cos(angle), jnp.sin(angle))


def rotate(values, cosine, sine):
    half = ROT // 2
    first = values[..., :half]
    second = values[..., half:ROT]
    cosine = cosine[:, None, :]
    sine = sine[:, None, :]
    return jnp.concatenate(
        [first * cosine - second * sine, second * cosine + first * sine, values[..., ROT:]], -1
    )


def exact_gelu(values):
    return jax.nn.gelu(values, approximate=False)


def shards(
    tokens,
    input_gain,
    input_bias,
    post_gain,
    post_bias,
    query_key_value,
    query_key_value_bias,
    dense_weight,
    dense_bias,
    expand_weight,
    expand_bias,
    contract_weight,
    contract_bias,
    lengths,
    cotangent,
):
    local_width = query_key_value.shape[2]
    local_heads = local_width // HD
    first_low, unit_one, inverse_one = normalize(tokens, input_gain, input_bias)
    second_low, unit_two, inverse_two = normalize(tokens, post_gain, post_bias)
    normed_one, normed_two = (
        lax.all_gather(first_low, "tensor", axis=0, tiled=True),
        lax.all_gather(second_low, "tensor", axis=0, tiled=True),
    )
    count = normed_one.shape[0]
    block = min(512, LEN)
    blocks = count // block
    per_sentence = LEN // block
    sentences = count // LEN
    scale = HD ** (-0.5)
    cosine, sine = angles(count)
    projected = (
        jnp.einsum("td,cdh->cth", normed_one, query_key_value, preferred_element_type=jnp.float32)
        + query_key_value_bias[:, None, :]
    )
    queries = rotate(projected[0].reshape(count, local_heads, HD), cosine, sine).astype(
        jnp.bfloat16
    )
    key_rows = rotate(projected[1].reshape(count, local_heads, HD), cosine, sine).astype(
        jnp.bfloat16
    )
    value_rows = projected[2].reshape(count, local_heads, HD).astype(jnp.bfloat16)
    key_place = jnp.arange(LEN)

    def prepare(index):
        which = index // per_sentence
        start = index * block
        query_block = lax.dynamic_slice_in_dim(queries, start, block, 0)
        query_place = start - which * LEN + jnp.arange(block)
        allowed = (key_place[None, :] <= query_place[:, None]) & (
            key_place[None, :] < lengths[which]
        )
        scores = (
            jnp.einsum("qhe,khe->hqk", query_block, key_rows, preferred_element_type=jnp.float32)
            * scale
        )
        scores = jnp.where(allowed[None], scores, MASKED)
        return (start, query_block, key_rows, value_rows, scores)

    def attend(index):
        start, query_block, key_block, value_block, scores = prepare(index)
        highest = jnp.max(scores, -1, keepdims=True)
        weights = jnp.exp(scores - highest)
        total = jnp.sum(weights, -1, keepdims=True)
        probs = (weights / total).astype(jnp.bfloat16)
        output = jnp.einsum("hqk,khe->qhe", probs, value_block, preferred_element_type=jnp.float32)
        return (output.astype(jnp.bfloat16), highest + jnp.log(total))

    context_blocks, log_totals = lax.map(attend, jnp.arange(blocks))
    context = context_blocks.reshape(count, local_width)
    pre_act = jnp.dot(normed_two, expand_weight, preferred_element_type=jnp.float32) + expand_bias
    activation_full, gelu_pull = jax.vjp(exact_gelu, pre_act)
    activation = activation_full.astype(jnp.bfloat16)
    context_rows = context
    active_rows = activation
    summed = lax.psum_scatter(
        jnp.dot(context_rows, dense_weight, preferred_element_type=jnp.float32)
        + jnp.dot(active_rows, contract_weight, preferred_element_type=jnp.float32),
        "tensor",
        scatter_dimension=0,
        tiled=True,
    )
    mixed = (tokens.astype(jnp.float32) + summed + dense_bias + contract_bias).astype(jnp.bfloat16)
    piece = lax.all_gather(cotangent, "tensor", axis=0, tiled=True)
    context_rows = context
    active_rows = activation
    grad_dense = jnp.einsum("tc,td->cd", context_rows, piece, preferred_element_type=jnp.float32)
    grad_contract = jnp.einsum("tf,td->fd", active_rows, piece, preferred_element_type=jnp.float32)
    grad_context = jnp.einsum("td,cd->tc", piece, dense_weight, preferred_element_type=jnp.float32)
    grad_active = jnp.einsum(
        "td,fd->tf", piece, contract_weight, preferred_element_type=jnp.float32
    )
    grad_dense, grad_contract, grad_context, grad_active = (
        grad_dense,
        grad_contract,
        grad_context,
        grad_active,
    )
    grad_pre = gelu_pull(grad_active)[0].astype(jnp.bfloat16)
    grad_expand = jnp.einsum("td,tf->df", normed_two, grad_pre, preferred_element_type=jnp.float32)
    grad_expand_bias = jnp.sum(grad_pre.astype(jnp.float32), 0)
    part_two = jnp.einsum("tf,df->td", grad_pre, expand_weight, preferred_element_type=jnp.float32)
    grad_output = grad_context.astype(jnp.bfloat16).reshape(count, local_heads, HD)

    def attend_back(item):
        index, log_total = item
        start, query_block, key_block, value_block, scores = prepare(index)
        probs = jnp.exp(scores - log_total)
        grad_block = lax.dynamic_slice_in_dim(grad_output, start, block, 0)
        grad_probs = jnp.einsum(
            "qhe,khe->hqk", grad_block, value_block, preferred_element_type=jnp.float32
        )
        inner = jnp.sum(probs * grad_probs, -1, keepdims=True)
        grad_scores = (probs * (grad_probs - inner)).astype(jnp.bfloat16)
        grad_query = (
            jnp.einsum("hqk,khe->qhe", grad_scores, key_block, preferred_element_type=jnp.float32)
            * scale
        )
        grad_key = (
            jnp.einsum("hqk,qhe->khe", grad_scores, query_block, preferred_element_type=jnp.float32)
            * scale
        )
        grad_value = jnp.einsum(
            "hqk,qhe->khe",
            probs.astype(jnp.bfloat16),
            grad_block,
            preferred_element_type=jnp.float32,
        )
        return (grad_query, grad_key, grad_value)

    query_parts, key_parts, value_parts = lax.map(attend_back, (jnp.arange(blocks), log_totals))
    grad_queries = query_parts.reshape(count, local_heads, HD)
    grad_keys = (
        key_parts.reshape(sentences, per_sentence, LEN, local_heads, HD)
        .sum(1)
        .reshape(count, local_heads, HD)
    )
    grad_values = (
        value_parts.reshape(sentences, per_sentence, LEN, local_heads, HD)
        .sum(1)
        .reshape(count, local_heads, HD)
    )
    grad_projected = jnp.stack(
        [
            rotate(grad_queries, cosine, -sine).reshape(count, local_width),
            rotate(grad_keys, cosine, -sine).reshape(count, local_width),
            grad_values.reshape(count, local_width),
        ]
    ).astype(jnp.bfloat16)
    grad_projection = jnp.einsum(
        "td,cth->cdh", normed_one, grad_projected, preferred_element_type=jnp.float32
    )
    grad_projection_bias = jnp.sum(grad_projected.astype(jnp.float32), 1)
    part_one = jnp.einsum(
        "cth,cdh->td", grad_projected, query_key_value, preferred_element_type=jnp.float32
    )
    grad_one, grad_two = (
        lax.psum_scatter(part_one, "tensor", scatter_dimension=0, tiled=True),
        lax.psum_scatter(part_two, "tensor", scatter_dimension=0, tiled=True),
    )
    grad_tokens = (
        cotangent.astype(jnp.float32)
        + norm_back(grad_one, unit_one, inverse_one, input_gain)
        + norm_back(grad_two, unit_two, inverse_two, post_gain)
    )
    shared = lax.psum(
        (
            jnp.sum(grad_one * unit_one, 0),
            jnp.sum(grad_one, 0),
            jnp.sum(grad_two * unit_two, 0),
            jnp.sum(grad_two, 0),
            jnp.sum(cotangent.astype(jnp.float32), 0),
        ),
        ("dp", "tensor"),
    )
    weight_sums = lax.psum(
        (
            grad_projection,
            grad_projection_bias,
            grad_dense,
            grad_expand,
            grad_expand_bias,
            grad_contract,
        ),
        "dp",
    )
    return (
        mixed,
        grad_tokens,
        shared[0],
        shared[1],
        shared[2],
        shared[3],
        weight_sums[0],
        weight_sums[1],
        weight_sums[2],
        shared[4],
        weight_sums[3],
        weight_sums[4],
        weight_sums[5],
        shared[4],
    )


def solution(mesh):
    in_specs = (
        P(("dp", "tensor"), None),
        P(),
        P(),
        P(),
        P(),
        P(None, None, "tensor"),
        P(None, "tensor"),
        P("tensor", None),
        P(),
        P(None, "tensor"),
        P("tensor"),
        P("tensor", None),
        P(),
        P("dp"),
        P(("dp", "tensor"), None),
    )
    out_specs = (
        P(("dp", "tensor"), None),
        P(("dp", "tensor"), None),
        P(),
        P(),
        P(),
        P(),
        P(None, None, "tensor"),
        P(None, "tensor"),
        P("tensor", None),
        P(),
        P(None, "tensor"),
        P("tensor"),
        P("tensor", None),
        P(),
    )
    return jax.shard_map(shards, mesh=mesh, in_specs=in_specs, out_specs=out_specs, check_vma=False)
```

profile of v0, /device:TPU:0, one launch (start us, length us, event | category | flops | bytes accessed | tf_op | source)
XLA Modules:
  0.0 821.6 jit_solution(11198946212813716435)
XLA Ops:
  15.6 28.8 %all-gather.4.cloned.1.call-done = bf16[2048,768]{1,0:T(8,128)(2,1)} async-done(((bf16[512,768]{1,0:T(8,128)(2,1)}), bf16[2048,768]{1,0:T(8,128)(2,1)}) %all-gather.4.cloned.1.call-update) | async-done | bytes 3145744 | tf_op jit(solution)/shard_map/all_gather | solution.py:77
  51.4 105.4 %while.34 = (s32[]{:T(128)}, bf16[4,512,3,64]{1,3,2,0:T(8,128)(2,1)}, f32[4,3,512,1]{2,1,3,0:T(4,128)S(1)}, s32[4]{0:T(128)S(1)}, s32[1]{0:T(128)}, /*index=5*/b...) while((s32[]{:T(128)}, ...), condition=%wide.region_5.6_spmd.clone.clone, body=%wide.region_2.5_spmd.clone.clone.sunk | while | flops 845251584 | bytes 47119264 | solution.py:124
  70.5 7.4 fusion.147
  96.8 7.4 fusion.147
  123.2 7.3 fusion.147
  160.8 198.1 %while.35 = (s32[]{:T(128)}, f32[4,512,3,64]{1,0,3,2:T(4,128)}, f32[4,2048,3,64]{1,3,2,0:T(8,128)}, f32[4,2048,3,64]{1,3,2,0:T(8,128)}, s32[4]{0:T(128)S(1)}, /*...) while((s32[]{:T(128)}, f32[4,512,3,64]{1,0,3,2:T(4,128)}, ...), condition=%wide.region_9.10_spmd.clone.clone, body=%wide.region_7.9_spmd.clone.clone.sunk | while | flops 2063041536 | bytes 160353760 | solution.py:186
  169.2 8.2 %multiply_reduce_fusion.4 = (f32[3,512]{1,0:T(4,128)S(1)}, f32[3,512,2048]{2,1,0:T(8,128)}) fusion(f32[3,512,2048]{2,1,0:T(8,128)S(1)} %fusion.157, f32[3,512]{1,0:T(4,128)S(1)} %dynamic-slice_bitcast_fusion.2, pred[512,2048]{1,0:T(8,128)(4,1)S(1)} %fusion.158, bf16[2048,3,64]{0,2,1:T(8,128)(2,1)S(1)} %copy-done.3, ...), kind=kOutput, calls=%fused_computation.22.clone.1 | convolution fusion | flops 418380288 | bytes 27209732 | tf_op jit(solution)/shard_map/while/body/eval_jaxpr/qhe,khe->hqk/dot_general | solution.py:165
  190.1 8.6 %dynamic_update_slice.57 = f32[4,512,3,64]{1,0,3,2:T(4,128)} dynamic-update-slice(f32[4,512,3,64]{1,0,3,2:T(4,128)} %get-tuple-element.664, f32[1,512,3,64]{1,0,3,2:T(1,128)S(1)} %copy.50, s32[]{:T(128)} %get-tuple-element.663, s32[]{:T(128)} %constant.209.clone.1..sunk.1, s32[]{:T(128)} %constant.209.clone.1..sunk.1, s32[]{:T(128)} %constant.209.clone.1..sunk.1) | dynamic-update-slice | bytes 786436 | tf_op jit(solution)/shard_map/while/body/jit(dynamic_update_index_in_dim)/dynamic_update_slice | solution.py:186
  198.7 9.3 %fusion.161 = f32[4,2048,3,64]{1,3,2,0:T(8,128)} fusion(f32[4,2048,3,64]{1,3,2,0:T(8,128)} %get-tuple-element.666, s32[]{:T(128)} %get-tuple-element.663, f32[3,512,2048]{2,1,0:T(8,128)} %copy-done.1, f32[3,512]{1,0:T(4,128)S(1)} %dynamic-slice_bitcast_fusion.2, pred[512,2048]{1,0:T(8,128)(4,1)S(1)} %fusion.158, ...), kind=kOutput, calls=%fused_computation.30.clone.1 | convolution fusion | flops 415236096 | bytes 15407620 | tf_op jit(solution)/shard_map/while/body/eval_jaxpr/hqk,qhe->khe/dot_general | solution.py:178
  216.1 8.2 %multiply_reduce_fusion.4 = (f32[3,512]{1,0:T(4,128)S(1)}, f32[3,512,2048]{2,1,0:T(8,128)}) fusion(f32[3,512,2048]{2,1,0:T(8,128)S(1)} %fusion.157, f32[3,512]{1,0:T(4,128)S(1)} %dynamic-slice_bitcast_fusion.2, pred[512,2048]{1,0:T(8,128)(4,1)S(1)} %fusion.158, bf16[2048,3,64]{0,2,1:T(8,128)(2,1)S(1)} %copy-done.3, ...), kind=kOutput, calls=%fused_computation.22.clone.1 | convolution fusion | flops 418380288 | bytes 27209732 | tf_op jit(solution)/shard_map/while/body/eval_jaxpr/qhe,khe->hqk/dot_general | solution.py:165
  237.0 8.6 %dynamic_update_slice.57 = f32[4,512,3,64]{1,0,3,2:T(4,128)} dynamic-update-slice(f32[4,512,3,64]{1,0,3,2:T(4,128)} %get-tuple-element.664, f32[1,512,3,64]{1,0,3,2:T(1,128)S(1)} %copy.50, s32[]{:T(128)} %get-tuple-element.663, s32[]{:T(128)} %constant.209.clone.1..sunk.1, s32[]{:T(128)} %constant.209.clone.1..sunk.1, s32[]{:T(128)} %constant.209.clone.1..sunk.1) | dynamic-update-slice | bytes 786436 | tf_op jit(solution)/shard_map/while/body/jit(dynamic_update_index_in_dim)/dynamic_update_slice | solution.py:186
  245.6 9.3 %fusion.161 = f32[4,2048,3,64]{1,3,2,0:T(8,128)} fusion(f32[4,2048,3,64]{1,3,2,0:T(8,128)} %get-tuple-element.666, s32[]{:T(128)} %get-tuple-element.663, f32[3,512,2048]{2,1,0:T(8,128)} %copy-done.1, f32[3,512]{1,0:T(4,128)S(1)} %dynamic-slice_bitcast_fusion.2, pred[512,2048]{1,0:T(8,128)(4,1)S(1)} %fusion.158, ...), kind=kOutput, calls=%fused_computation.30.clone.1 | convolution fusion | flops 415236096 | bytes 15407620 | tf_op jit(solution)/shard_map/while/body/eval_jaxpr/hqk,qhe->khe/dot_general | solution.py:178
  263.0 8.2 %multiply_reduce_fusion.4 = (f32[3,512]{1,0:T(4,128)S(1)}, f32[3,512,2048]{2,1,0:T(8,128)}) fusion(f32[3,512,2048]{2,1,0:T(8,128)S(1)} %fusion.157, f32[3,512]{1,0:T(4,128)S(1)} %dynamic-slice_bitcast_fusion.2, pred[512,2048]{1,0:T(8,128)(4,1)S(1)} %fusion.158, bf16[2048,3,64]{0,2,1:T(8,128)(2,1)S(1)} %copy-done.3, ...), kind=kOutput, calls=%fused_computation.22.clone.1 | convolution fusion | flops 418380288 | bytes 27209732 | tf_op jit(solution)/shard_map/while/body/eval_jaxpr/qhe,khe->hqk/dot_general | solution.py:165
  283.9 8.6 %dynamic_update_slice.57 = f32[4,512,3,64]{1,0,3,2:T(4,128)} dynamic-update-slice(f32[4,512,3,64]{1,0,3,2:T(4,128)} %get-tuple-element.664, f32[1,512,3,64]{1,0,3,2:T(1,128)S(1)} %copy.50, s32[]{:T(128)} %get-tuple-element.663, s32[]{:T(128)} %constant.209.clone.1..sunk.1, s32[]{:T(128)} %constant.209.clone.1..sunk.1, s32[]{:T(128)} %constant.209.clone.1..sunk.1) | dynamic-update-slice | bytes 786436 | tf_op jit(solution)/shard_map/while/body/jit(dynamic_update_index_in_dim)/dynamic_update_slice | solution.py:186
  292.5 9.3 %fusion.161 = f32[4,2048,3,64]{1,3,2,0:T(8,128)} fusion(f32[4,2048,3,64]{1,3,2,0:T(8,128)} %get-tuple-element.666, s32[]{:T(128)} %get-tuple-element.663, f32[3,512,2048]{2,1,0:T(8,128)} %copy-done.1, f32[3,512]{1,0:T(4,128)S(1)} %dynamic-slice_bitcast_fusion.2, pred[512,2048]{1,0:T(8,128)(4,1)S(1)} %fusion.158, ...), kind=kOutput, calls=%fused_computation.30.clone.1 | convolution fusion | flops 415236096 | bytes 15407620 | tf_op jit(solution)/shard_map/while/body/eval_jaxpr/hqk,qhe->khe/dot_general | solution.py:178
  309.9 8.2 %multiply_reduce_fusion.4 = (f32[3,512]{1,0:T(4,128)S(1)}, f32[3,512,2048]{2,1,0:T(8,128)}) fusion(f32[3,512,2048]{2,1,0:T(8,128)S(1)} %fusion.157, f32[3,512]{1,0:T(4,128)S(1)} %dynamic-slice_bitcast_fusion.2, pred[512,2048]{1,0:T(8,128)(4,1)S(1)} %fusion.158, bf16[2048,3,64]{0,2,1:T(8,128)(2,1)S(1)} %copy-done.3, ...), kind=kOutput, calls=%fused_computation.22.clone.1 | convolution fusion | flops 418380288 | bytes 27209732 | tf_op jit(solution)/shard_map/while/body/eval_jaxpr/qhe,khe->hqk/dot_general | solution.py:165
  330.7 8.6 %dynamic_update_slice.57 = f32[4,512,3,64]{1,0,3,2:T(4,128)} dynamic-update-slice(f32[4,512,3,64]{1,0,3,2:T(4,128)} %get-tuple-element.664, f32[1,512,3,64]{1,0,3,2:T(1,128)S(1)} %copy.50, s32[]{:T(128)} %get-tuple-element.663, s32[]{:T(128)} %constant.209.clone.1..sunk.1, s32[]{:T(128)} %constant.209.clone.1..sunk.1, s32[]{:T(128)} %constant.209.clone.1..sunk.1) | dynamic-update-slice | bytes 786436 | tf_op jit(solution)/shard_map/while/body/jit(dynamic_update_index_in_dim)/dynamic_update_slice | solution.py:186
  339.3 9.3 %fusion.161 = f32[4,2048,3,64]{1,3,2,0:T(8,128)} fusion(f32[4,2048,3,64]{1,3,2,0:T(8,128)} %get-tuple-element.666, s32[]{:T(128)} %get-tuple-element.663, f32[3,512,2048]{2,1,0:T(8,128)} %copy-done.1, f32[3,512]{1,0:T(4,128)S(1)} %dynamic-slice_bitcast_fusion.2, pred[512,2048]{1,0:T(8,128)(4,1)S(1)} %fusion.158, ...), kind=kOutput, calls=%fused_computation.30.clone.1 | convolution fusion | flops 415236096 | bytes 15407620 | tf_op jit(solution)/shard_map/while/body/eval_jaxpr/hqk,qhe->khe/dot_general | solution.py:178
  388.9 19.1 %convert_reduce_fusion = (f32[768]{0:T(1024)}, bf16[2048,768]{1,0:T(8,128)(2,1)S(1)}, f32[2048,768]{1,0:T(8,128)}) fusion(f32[2048,768]{1,0:T(8,128)S(1)} %fusion.88, f32[768]{0:T(1024)S(1)} %copy-done.26, bf16[2048,768]{1,0:T(8,128)(2,1)S(1)} %copy-done.7, bf16[768,768]{1,0:T(8,128)(2,1)S(1)} %copy-done), kind=kOutput, calls=%fused_computation.53 | convolution fusion | flops 2533883136 | bytes 20060160 | tf_op jit(solution)/shard_map/td,fd->tf/dot_general | solution.py:145
  448.1 22.3 %all-reduce.1 = (f32[3,192]{1,0:T(4,128)}, f32[768]{0:T(1024)}) all-reduce(f32[3,192]{1,0:T(4,128)} %convert_reduce_fusion.1, f32[768]{0:T(1024)} %get-tuple-element.445), channel_id=1, replica_groups=mesh['dp'=8,'tensor'=4] {'dp'}, use_global_device_ids=true, to_apply=%region_28.29 | all-reduce | flops 1344 | bytes 10752 | tf_op jit(solution)/shard_map/psum | solution.py:231
  470.4 31.9 %reduce-scatter.8.cloned.1.call-done = f32[512,768]{1,0:T(8,128)} async-done(((f32[2048,768]{1,0:T(8,128)}), f32[512,768]{1,0:T(8,128)}) %reduce-scatter.8.cloned.1.call-update) | async-done | bytes 1572880 | tf_op jit(solution)/shard_map/reduce_scatter | solution.py:214
  508.3 54.8 %reduce-scatter.4.cloned.1.call-done = f32[512,768]{1,0:T(8,128)} async-done(((f32[2048,768]{1,0:T(8,128)}), f32[512,768]{1,0:T(8,128)}) %reduce-scatter.4.cloned.1.call-update) | async-done | bytes 1572880 | tf_op jit(solution)/shard_map/reduce_scatter | solution.py:131
  567.6 43.6 %all-reduce = (f32[768]{0:T(1024)}, f32[768]{0:T(1024)}, f32[768]{0:T(1024)}, f32[768]{0:T(1024)}, f32[768]{0:T(1024)S(1)}) all-reduce(f32[768]{0:T(1024)} %get-tuple-element.386, f32[768]{0:T(1024)} %get-tuple-element.391, f32[768]{0:T(1024)} %get-tuple-element.395, ...), channel_id=1, replica_groups=mesh['dp'=8,'tensor'=4] {'dp','tensor'}, use_global_device_ids=true, to_apply=%region_19.20 | all-reduce | flops 3840 | bytes 30720 | tf_op jit(solution)/shard_map/psum | solution.py:221
  611.2 194.9 %all-reduce.5.cloned.1.call-done = (f32[3,768,192]{1,2,0:T(8,128)}, f32[192,768]{1,0:T(8,128)}, f32[768,768]{1,0:T(8,128)}, f32[768,768]{1,0:T(8,128)}) async-done(((f32[3,768,192]{1,2,0:T(8,128)}, f32[192,768]{1,0:T(8,128)}, f32[768,768]{1,0:T(8,128)}, f32[768,768]{1,0:T(8,128)}), (f32[3,768,192]{1,2,0:T(8,128)}, f32[192,768]{1,0:T(8,128)}, f32[768,768]{1,0:T(8,128)}, ...) | async-done | bytes 7077904 | tf_op jit(solution)/shard_map/psum | solution.py:231
  (226 shorter events, 247.6 us)
Async XLA Ops:
  7.2 381.7 %copy-start = (bf16[768,768]{1,0:T(8,128)(2,1)S(1)}, bf16[768,768]{1,0:T(8,128)(2,1)}, u32[]{:S(2)}) copy-start(bf16[768,768]{1,0:T(8,128)(2,1)} %param.30) | copy-start | bytes 3538948
  7.2 37.3 %copy-start.30 = (bf16[3,768,192]{1,2,0:T(8,128)(2,1)S(1)}, bf16[3,768,192]{1,2,0:T(8,128)(2,1)}, u32[]{:S(2)}) copy-start(bf16[3,768,192]{1,2,0:T(8,128)(2,1)} %param.24) | copy-start | bytes 2654212
  7.2 37.3 %all-gather.4.cloned.1.call-start = ((), (), s32[]{:S(2)}) async-start(), calls=%async_computation.3 | async-start | bytes 3932160 | tf_op jit(solution)/shard_map/all_gather | solution.py:77
  13.1 143.7 %all-gather.8.cloned.1.call-start = ((), (), s32[]{:S(2)}) async-start(), calls=%async_computation.6 | async-start | bytes 3932160 | tf_op jit(solution)/shard_map/all_gather | solution.py:139
  13.8 369.1 %all-gather.6.cloned.1.call-start = ((), (), s32[]{:S(2)}) async-start(), calls=%async_computation.4 | async-start | bytes 3932160 | tf_op jit(solution)/shard_map/all_gather | solution.py:78
  14.6 455.8 %reduce-scatter.6.cloned.1.call-start = ((), (), s32[]{:S(2)}) async-start(), calls=%async_computation.7 | async-start | bytes 7864320 | tf_op jit(solution)/shard_map/reduce_scatter | solution.py:213
  15.6 34.7 %copy-start.16 = (f32[2048,8]{0,1:T(8,128)}, f32[2048,8]{0,1:T(8,128)S(1)}, u32[]{:S(2)}) copy-start(f32[2048,8]{0,1:T(8,128)S(1)} %get-tuple-element.473) | copy-start | bytes 196612
  51.4 105.4 %copy-start.17 = (bf16[192,768]{1,0:T(8,128)(2,1)S(1)}, bf16[192,768]{1,0:T(8,128)(2,1)}, u32[]{:S(2)}) copy-start(bf16[192,768]{1,0:T(8,128)(2,1)} %param.26) | copy-start | bytes 884740
  63.6 6.9 copy-start.2
  169.1 8.3 %copy-start.1 = (f32[3,512,2048]{2,1,0:T(8,128)}, f32[3,512,2048]{2,1,0:T(8,128)S(1)}, u32[]{:S(2)}) copy-start(f32[3,512,2048]{2,1,0:T(8,128)S(1)} %fusion.157) | copy-start | bytes 37748740 | tf_op jit(solution)/shard_map/while
  216.1 8.3 %copy-start.1 = (f32[3,512,2048]{2,1,0:T(8,128)}, f32[3,512,2048]{2,1,0:T(8,128)S(1)}, u32[]{:S(2)}) copy-start(f32[3,512,2048]{2,1,0:T(8,128)S(1)} %fusion.157) | copy-start | bytes 37748740 | tf_op jit(solution)/shard_map/while
  263.0 8.3 %copy-start.1 = (f32[3,512,2048]{2,1,0:T(8,128)}, f32[3,512,2048]{2,1,0:T(8,128)S(1)}, u32[]{:S(2)}) copy-start(f32[3,512,2048]{2,1,0:T(8,128)S(1)} %fusion.157) | copy-start | bytes 37748740 | tf_op jit(solution)/shard_map/while
  309.9 8.3 %copy-start.1 = (f32[3,512,2048]{2,1,0:T(8,128)}, f32[3,512,2048]{2,1,0:T(8,128)S(1)}, u32[]{:S(2)}) copy-start(f32[3,512,2048]{2,1,0:T(8,128)S(1)} %fusion.157) | copy-start | bytes 37748740 | tf_op jit(solution)/shard_map/while
  382.9 119.5 %reduce-scatter.8.cloned.1.call-start = ((), (), s32[]{:S(2)}) async-start(), calls=%async_computation.8 | async-start | bytes 7864320 | tf_op jit(solution)/shard_map/reduce_scatter | solution.py:214
  388.9 19.1 %copy-start.5 = (f32[2048,768]{1,0:T(8,128)}, f32[2048,768]{1,0:T(8,128)S(1)}, u32[]{:S(2)}) copy-start(f32[2048,768]{1,0:T(8,128)S(1)} %fusion.88) | copy-start | bytes 18874372
  414.2 148.9 %reduce-scatter.4.cloned.1.call-start = ((), (), s32[]{:S(2)}) async-start(), calls=%async_computation.5 | async-start | bytes 7864320 | tf_op jit(solution)/shard_map/reduce_scatter | solution.py:131
  428.2 377.9 %all-reduce.5.cloned.1.call-start = ((), (), s32[]{:S(2)}) async-start(), calls=%async_computation.9 | async-start | bytes 14155776 | tf_op jit(solution)/shard_map/psum | solution.py:231
  445.9 56.4 %copy-start.4 = (bf16[512,768]{1,0:T(8,128)(2,1)S(1)}, bf16[512,768]{1,0:T(8,128)(2,1)}, u32[]{:S(2)}) copy-start(bf16[512,768]{1,0:T(8,128)(2,1)} %param.19) | copy-start | bytes 2359300
  445.9 56.4 %copy-start.20 = (f32[512]{0:T(512)S(1)}, f32[512]{0:T(512)}, u32[]{:S(2)}) copy-start(f32[512]{0:T(512)} %copy-done.19) | copy-start | bytes 6148
  445.9 56.4 %copy-start.21 = (f32[768]{0:T(1024)S(1)}, f32[768]{0:T(1024)}, u32[]{:S(2)}) copy-start(f32[768]{0:T(1024)} %param.20) | copy-start | bytes 9220
  445.9 56.4 %copy-start.22 = (f32[768]{0:T(1024)S(1)}, f32[768]{0:T(1024)}, u32[]{:S(2)}) copy-start(f32[768]{0:T(1024)} %param.22) | copy-start | bytes 9220
  445.9 56.4 %copy-start.24 = (f32[512]{0:T(512)S(1)}, f32[512]{0:T(512)}, u32[]{:S(2)}) copy-start(f32[512]{0:T(512)} %copy-done.23) | copy-start | bytes 6148
  470.4 92.8 %copy-start.6 = (f32[512,768]{1,0:T(8,128)S(1)}, f32[512,768]{1,0:T(8,128)}, u32[]{:S(2)}) copy-start(f32[512,768]{1,0:T(8,128)} %reduce-scatter.6.cloned.1.call-done) | copy-start | bytes 4718596
  611.2 201.8 %copy-start.27 = (f32[768]{0:T(1024)}, f32[768]{0:T(1024)S(1)}, u32[]{:S(2)}) copy-start(f32[768]{0:T(1024)S(1)} %get-tuple-element.736) | copy-start | bytes 9220
  (25 other events, 97.0 us)
Sparse Core Ops, SparseCore 0:
  13.2 31.2 all-gather.3
  46.0 28.5 all-gather.7
  76.7 28.5 all-gather.5
  383.0 58.3 reduce-scatter.5
  443.9 58.3 reduce-scatter.7
  504.7 58.3 reduce-scatter.3
  569.4 236.6 all-reduce.4
where the time goes:
time: 832 us; the launch traced here: 822 us
  waiting for transfers between devices  312 us (38%)
  matrix products  225 us (27%)
  other arithmetic  104 us (12%)
  blocking collectives  65.9 us (8%)
  local copies, waits for them, and re-layouts  61.8 us (7%)
  loops' own time  37.1 us (4%)
  between operations  14.9 us (2%)
    psum x1, waiting for transfers between devices, shards(): lax.psum((grad_projection, grad_projection_bias, grad_dense, grad_expand,...  195 us
    reduce_scatter x1, waiting for transfers between devices, shards(): lax.psum_scatter(jnp.dot(context_rows, dense_weight, preferred_element_ty...  54.8 us
    psum x1, blocking collectives, shards(): lax.psum((jnp.sum(grad_one * unit_one, 0), jnp.sum(grad_one, 0), jnp.sum(...  43.6 us
    dot_general x8, matrix products, prepare(): jnp.einsum('qhe,khe->hqk', query_block, key_rows, preferred_element_type=...  38.7 us
    dot_general x4, matrix products, attend_back(): jnp.einsum('hqk,qhe->khe', probs.astype(jnp.bfloat16), grad_block, prefer...  37.2 us
    dynamic_update_slice x8, local copies, waits for them, and re-layouts, shards(): lax.map(attend_back, (jnp.arange(blocks), log_totals))  36.1 us
    dot_general x4, matrix products, attend_back(): jnp.einsum('qhe,khe->hqk', grad_block, value_block, preferred_element_typ...  32.9 us
    reduce_scatter x1, waiting for transfers between devices, shards(): lax.psum_scatter(part_two, 'tensor', scatter_dimension=0, tiled=True)  31.9 us
  transfers between devices with their start and end apart: 7, of which 4 were waited for; matrix products, arithmetic and copies ran while one was open for 45% of the time, Pallas kernels for 0%

commit v1 on v0

v1 whole, which is shorter than its diff:
```python
import functools

import jax
import jax.numpy as jnp
import numpy as np
from jax import lax
from jax.experimental import pallas as pl
from jax.experimental.pallas import tpu as pltpu
from jax.sharding import PartitionSpec as P

HD = 64
ROT = 16
LEN = 2048
EPS = 1e-05
MASKED = -1e30
F32 = jnp.float32
BF16 = jnp.bfloat16


def dot(a, b, ca, cb):
    return lax.dot_general(a, b, (((ca,), (cb,)), ((), ())), preferred_element_type=F32)


def angle_rows(count):
    half = ROT // 2
    freqs = np.float32(10000.0) ** (
        np.float32(-2.0) * np.arange(half, dtype=np.float32) / np.float32(ROT)
    )
    place = (np.arange(count) % LEN).astype(np.float32)
    angle = (freqs[:, None] * place[None, :]).astype(np.float32)
    return np.cos(angle), np.sin(angle)


def unit_rows(rows):
    values = rows.astype(F32)
    centred = values - jnp.mean(values, -1, keepdims=True)
    inverse = lax.rsqrt(jnp.mean(centred * centred, -1, keepdims=True) + EPS)
    return centred * inverse, inverse


def core(
    blk,
    x_ref,
    g_ref,
    len_ref,
    gain1,
    bias1,
    gain2,
    bias2,
    wt,
    qkv_b,
    wd,
    we,
    exp_b,
    wc,
    cos_t,
    sin_t,
    mix_o,
    s_o,
    dwt,
    dwd,
    dwe,
    dwc,
    vec_o,
    dbe,
    dbq,
    n1_s,
    qa,
    kt,
    kr,
    va,
    vr,
    dot_s,
    sc,
    pt,
    dkt,
    dvt,
    ctx_s,
    gp,
    dq_s,
):
    total, width = x_ref.shape
    local = wd.shape[0]
    heads = local // HD
    count = total // blk
    per = LEN // blk
    root = HD**-0.5

    for ref in (dwt, dwd, dwe, dwc, vec_o, dbe, dbq, dkt, dvt):
        ref[...] = jnp.zeros_like(ref)
    one_row = (lax.broadcasted_iota(jnp.int32, (heads, HD, total), 1) == 0).astype(F32)
    qa[:, HD:, :] = one_row.astype(BF16)
    va[:, HD:, :] = one_row[:, : va.shape[1] - HD, :].astype(BF16)

    def dense(b, _):
        rows = pl.ds(pl.multiple_of(b * blk, blk), blk)
        unit, _inv = unit_rows(x_ref[rows, :])
        n1 = (unit * gain1[...] + bias1[...]).astype(BF16)
        n2 = (unit * gain2[...] + bias2[...]).astype(BF16)
        n1_s[rows, :] = n1
        g = g_ref[rows, :]
        proj = dot(wt[...], n1, 1, 1) + qkv_b[...]
        cosine = cos_t[:, rows]
        sine = sin_t[:, rows]

        def turn(block):
            a = block[: ROT // 2]
            c = block[ROT // 2 : ROT]
            return jnp.concatenate(
                [a * cosine - c * sine, c * cosine + a * sine, block[ROT:]], 0
            )

        place = lax.broadcasted_iota(jnp.int32, (HD, blk), 1) + lax.rem(b, per) * blk
        first = lax.broadcasted_iota(jnp.int32, (HD, blk), 0) == 0
        extra = jnp.where(first & (place >= len_ref[b // per]), MASKED, 0.0)
        for h in range(heads):
            lo = h * HD
            q = turn(proj[lo : lo + HD])
            k = turn(proj[local + lo : local + lo + HD])
            v = proj[2 * local + lo : 2 * local + lo + HD]
            qa[h, :HD, rows] = (q * root).astype(BF16)
            kt[h, :, rows] = k.astype(BF16)
            kr[h, rows, :] = jnp.transpose(jnp.concatenate([k, extra], 0)).astype(BF16)
            va[h, :HD, rows] = v.astype(BF16)
            vr[h, rows, :] = jnp.transpose(v).astype(BF16)
        grad_ctx = dot(wd[...], g, 1, 1).astype(BF16)
        for h in range(heads):
            dot_s[h, :, rows] = grad_ctx[h * HD : (h + 1) * HD]
        pre = dot(n2, we[...], 1, 0) + exp_b[...]
        big = 0.5 * (1.0 + lax.erf(pre * np.float32(0.5**0.5)))
        act = (pre * big).astype(BF16)
        slope = big + pre * (jnp.exp(-0.5 * pre * pre) * np.float32((2 * np.pi) ** -0.5))
        mix_o[rows, :] = dot(act, wc[...], 1, 0).astype(BF16)
        dwc[...] += dot(act, g, 0, 0)
        grad_pre_f = dot(g, wc[...], 1, 1) * slope
        grad_pre = grad_pre_f.astype(BF16)
        dbe[...] += jnp.sum(grad_pre.astype(F32), 0, keepdims=True)
        dwe[...] += dot(n2, grad_pre, 0, 0)
        part = dot(grad_pre, we[...], 1, 1)
        s_o[rows, :] = (part * gain2[...]).astype(BF16)
        vec_o[2:3, :] += jnp.sum(part * unit, 0, keepdims=True)
        vec_o[3:4, :] += jnp.sum(part, 0, keepdims=True)
        return 0

    lax.fori_loop(0, count, dense, 0)

    key_i = lax.broadcasted_iota(jnp.int32, (blk, blk), 0)
    query_i = lax.broadcasted_iota(jnp.int32, (blk, blk), 1)

    def attend(step, _):
        i = count - 1 - step
        base = (i // per) * per
        mine = pl.ds(pl.multiple_of(i * blk, blk), blk)

        def head(h, _):
            q_aug = qa[h, :, mine]

            def score(j, high):
                cols = pl.ds(pl.multiple_of(j * blk, blk), blk)
                s = dot(kr[h, cols, :], q_aug, 1, 0)
                sc[pl.ds(pl.multiple_of((j - base) * blk, blk), blk), :] = s
                return jnp.maximum(high, jnp.max(s.reshape(blk // 8, 8, blk), 0))

            high = lax.fori_loop(base, i, score, jnp.full((8, blk), MASKED, F32))
            s = dot(kr[h, mine, :], q_aug, 1, 0)
            s = jnp.where(key_i <= query_i, s, MASKED)
            sc[pl.ds(pl.multiple_of((i - base) * blk, blk), blk), :] = s
            high = jnp.maximum(high, jnp.max(s.reshape(blk // 8, 8, blk), 0))
            high = jnp.max(high, 0, keepdims=True)

            def weigh(j, out):
                cols = pl.ds(pl.multiple_of(j * blk, blk), blk)
                here = pl.ds(pl.multiple_of((j - base) * blk, blk), blk)
                p = jnp.exp(sc[here, :] - high).astype(BF16)
                pt[here, :] = p
                return out + dot(va[h, :, cols], p, 1, 0)

            out = lax.fori_loop(base, i + 1, weigh, jnp.zeros((va.shape[1], blk), F32))
            scale = 1.0 / out[HD : HD + 1]
            ctx = out[:HD] * scale
            ctx_s[h] = ctx.astype(BF16)
            go = (dot_s[h, :, mine].astype(F32) * scale).astype(BF16)
            inner = jnp.sum(ctx * go.astype(F32), 0, keepdims=True)
            q = q_aug[:HD]

            def back(j, dq):
                cols = pl.ds(pl.multiple_of(j * blk, blk), blk)
                here = pl.ds(pl.multiple_of((j - base) * blk, blk), blk)
                p = pt[here, :]
                dvt[h, :, cols] += dot(go, p, 1, 1)
                dp = dot(vr[h, cols, :], go, 1, 0)
                ds = (p.astype(F32) * (dp - inner)).astype(BF16)
                dkt[h, :, cols] += dot(q, ds, 1, 1)
                return dq + dot(kt[h, :, cols], ds, 1, 0)

            dq_s[h] = lax.fori_loop(base, i + 1, back, jnp.zeros((HD, blk), F32))
            return 0

        lax.fori_loop(0, heads, head, 0)
        cosine = cos_t[:, mine]
        sine = sin_t[:, mine]

        def unturn(block):
            a = block[: ROT // 2]
            c = block[ROT // 2 : ROT]
            return jnp.concatenate(
                [a * cosine + c * sine, c * cosine - a * sine, block[ROT:]], 0
            )

        for h in range(heads):
            lo = h * HD
            gp[lo : lo + HD, :] = unturn(dq_s[h] * root).astype(BF16)
            gp[local + lo : local + lo + HD, :] = unturn(dkt[h, :, mine]).astype(BF16)
            gp[2 * local + lo : 2 * local + lo + HD, :] = dvt[h, :, mine].astype(BF16)
        grad_proj = gp[...]
        ctx_all = ctx_s[...].reshape(local, blk)
        mix = dot(ctx_all, wd[...], 0, 0) + mix_o[mine, :].astype(F32)
        mix_o[mine, :] = mix.astype(BF16)
        dwd[...] += dot(ctx_all, g_ref[mine, :], 1, 0)
        dwt[...] += dot(grad_proj, n1_s[mine, :], 1, 0)
        part = dot(grad_proj, wt[...], 0, 0) * gain1[...] + s_o[mine, :].astype(F32)
        s_o[mine, :] = part.astype(BF16)
        dbq[...] += jnp.sum(grad_proj.astype(F32), 1, keepdims=True)
        return 0

    lax.fori_loop(0, count, attend, 0)
    w32 = wt[...].astype(F32)
    grad_bias = jnp.sum(w32 * dbq[...], 0, keepdims=True)
    vec_o[1:2, :] = grad_bias
    vec_o[0:1, :] = (jnp.sum(w32 * dwt[...], 0, keepdims=True) - bias1[...] * grad_bias) / gain1[
        ...
    ]


def shards(
    tokens,
    input_gain,
    input_bias,
    post_gain,
    post_bias,
    query_key_value,
    query_key_value_bias,
    dense_weight,
    dense_bias,
    expand_weight,
    expand_bias,
    contract_weight,
    contract_bias,
    lengths,
    cotangent,
):
    width = tokens.shape[1]
    local = query_key_value.shape[2]
    heads = local // HD
    hidden = expand_weight.shape[1]
    blk = tokens.shape[0]
    x = lax.all_gather(tokens, "tensor", axis=0, tiled=True)
    g = lax.all_gather(cotangent, "tensor", axis=0, tiled=True)
    total = x.shape[0]
    wt = jnp.transpose(query_key_value, (0, 2, 1)).reshape(3 * local, width)
    cosine, sine = angle_rows(total)
    vmem = pl.BlockSpec(memory_space=pltpu.VMEM)
    smem = pl.BlockSpec(memory_space=pltpu.SMEM)
    outs = pl.pallas_call(
        functools.partial(core, blk),
        name="core",
        out_shape=(
            jax.ShapeDtypeStruct((total, width), BF16),
            jax.ShapeDtypeStruct((total, width), BF16),
            jax.ShapeDtypeStruct((3 * local, width), F32),
            jax.ShapeDtypeStruct((local, width), F32),
            jax.ShapeDtypeStruct((width, hidden), F32),
            jax.ShapeDtypeStruct((hidden, width), F32),
            jax.ShapeDtypeStruct((8, width), F32),
            jax.ShapeDtypeStruct((1, hidden), F32),
            jax.ShapeDtypeStruct((3 * local, 1), F32),
        ),
        in_specs=[vmem, vmem, smem] + [vmem] * 12,
        out_specs=[vmem] * 9,
        scratch_shapes=[
            pltpu.VMEM((total, width), BF16),
            pltpu.VMEM((heads, 2 * HD, total), BF16),
            pltpu.VMEM((heads, HD, total), BF16),
            pltpu.VMEM((heads, total, 2 * HD), BF16),
            pltpu.VMEM((heads, HD + 16, total), BF16),
            pltpu.VMEM((heads, total, HD), BF16),
            pltpu.VMEM((heads, HD, total), BF16),
            pltpu.VMEM((LEN, blk), F32),
            pltpu.VMEM((LEN, blk), BF16),
            pltpu.VMEM((heads, HD, total), F32),
            pltpu.VMEM((heads, HD, total), F32),
            pltpu.VMEM((heads, HD, blk), BF16),
            pltpu.VMEM((3 * local, blk), BF16),
            pltpu.VMEM((heads, HD, blk), F32),
        ],
        compiler_params=pltpu.CompilerParams(vmem_limit_bytes=62 * 2**20),
    )(
        x,
        g,
        lengths,
        input_gain[None],
        input_bias[None],
        post_gain[None],
        post_bias[None],
        wt,
        query_key_value_bias.reshape(3 * local, 1),
        dense_weight,
        expand_weight,
        expand_bias[None],
        contract_weight,
        cosine,
        sine,
    )
    mix_p, s_p, dwt, dwd, dwe, dwc, vec, dbe, dbq = outs
    mix = lax.psum_scatter(mix_p, "tensor", scatter_dimension=0, tiled=True)
    grad_s = lax.psum_scatter(s_p, "tensor", scatter_dimension=0, tiled=True).astype(F32)
    mixed = (
        tokens.astype(F32) + mix.astype(F32) + dense_bias + contract_bias
    ).astype(BF16)
    unit, inverse = unit_rows(tokens)
    grad_tokens = cotangent.astype(F32) + inverse * (
        grad_s
        - jnp.mean(grad_s, -1, keepdims=True)
        - unit * jnp.mean(grad_s * unit, -1, keepdims=True)
    )
    vec = vec.at[4].set(jnp.sum(cotangent.astype(F32), 0))
    vec = lax.psum(vec, ("dp", "tensor"))
    small = lax.psum((dbe, dbq), "dp")
    grads = lax.psum(
        (dwt.astype(BF16), dwd.astype(BF16), dwe.astype(BF16), dwc.astype(BF16)), "dp"
    )
    grad_qkv = jnp.transpose(grads[0].astype(F32).reshape(3, local, width), (0, 2, 1))
    return (
        mixed,
        grad_tokens,
        vec[0],
        vec[1],
        vec[2],
        vec[3],
        grad_qkv,
        small[1].reshape(3, local),
        grads[1].astype(F32),
        vec[4],
        grads[2].astype(F32),
        small[0][0],
        grads[3].astype(F32),
        vec[4],
    )


def solution(mesh):
    rows = P(("dp", "tensor"), None)
    weights = (
        P(None, None, "tensor"),
        P(None, "tensor"),
        P("tensor", None),
        P(),
        P(None, "tensor"),
        P("tensor"),
        P("tensor", None),
        P(),
    )
    return jax.shard_map(
        shards,
        mesh=mesh,
        in_specs=(rows, P(), P(), P(), P()) + weights + (P("dp"), rows),
        out_specs=(rows, rows, P(), P(), P(), P()) + weights,
        check_vma=False,
    )
```

time: 832 us -> 426 us (0.51); the launches traced: 822 us -> 426 us
  matrix products: 225 us -> 0 us
  other arithmetic: 104 us -> 18.6 us
  Pallas kernels: 0 us -> 76.2 us
  waiting for transfers between devices: 312 us -> 246 us
  local copies, waits for them, and re-layouts: 61.8 us -> 7.08 us
  loops' own time: 37.1 us -> 0 us
    dot_general x39 -> x0, matrix products: 221 us -> none  [the longest x8 38.7 us: prepare(): jnp.einsum('qhe,khe->hqk', query_block, key_rows, preferred_element_type=...]
    psum x1, waiting for transfers between devices: 195 us -> 115 us  [shards(): lax.psum((dwt.astype(BF16), dwd.astype(BF16), dwe.astype(BF16), dwc.astyp...]
    pallas_call x0 -> x1, Pallas kernels: none -> 76.2 us  [shards(): pl.pallas_call(functools.partial(core, blk), name='core', out_shape=(jax....]
    reduce_sum x11 -> x4, other arithmetic: 48.7 us -> 5.84 us  [the longest x1 3.37 us: shards(): vec = vec.at[4].set(jnp.sum(cotangent.astype(F32), 0))]
    another operation x2 -> x0, loops' own time: 37.1 us -> none  [the longest x1 23.8 us: shards(): lax.map(attend_back, (jnp.arange(blocks), log_totals))]
    dynamic_update_slice x8 -> x0, local copies, waits for them, and re-layouts: 36.1 us -> none  [shards(): lax.map(attend_back, (jnp.arange(blocks), log_totals))]
    all_gather x3 -> x2, waiting for transfers between devices: 28.9 us -> 57.7 us  [the longest x1 30.1 us: shards(): g = lax.all_gather(cotangent, 'tensor', axis=0, tiled=True)]
    convert_element_type x7, other arithmetic: 35.7 us -> 11.2 us  [the longest x1 2.95 us: shards(): dwe.astype(BF16)]
  transfers between devices with their start and end apart: 7 -> 5, of which waited for: 4 -> 5; matrix products, arithmetic and copies ran while one was open for 45% -> 3% of each run, Pallas kernels for 0% -> 0%
where the time goes in v1:
time: 426 us
  waiting for transfers between devices  246 us (58%)
  Pallas kernels  76.2 us (18%)
  blocking collectives  62.9 us (15%)
  other arithmetic  18.6 us (4%)
  between operations  14.6 us (3%)
  local copies, waits for them, and re-layouts  7.08 us (2%)
    psum x1, waiting for transfers between devices, shards(): lax.psum((dwt.astype(BF16), dwd.astype(BF16), dwe.astype(BF16), dwc.astyp...  115 us
    pallas_call x1, Pallas kernels, shards(): pl.pallas_call(functools.partial(core, blk), name='core', out_shape=(jax....  76.2 us
    psum x1, blocking collectives, shards(): vec = lax.psum(vec, ('dp', 'tensor'))  39.5 us
    reduce_scatter x1, waiting for transfers between devices, shards(): mix = lax.psum_scatter(mix_p, 'tensor', scatter_dimension=0, tiled=True)  38.4 us
    reduce_scatter x1, waiting for transfers between devices, shards(): lax.psum_scatter(s_p, 'tensor', scatter_dimension=0, tiled=True).astype(F32)  32.7 us
    all_gather x1, waiting for transfers between devices, shards(): g = lax.all_gather(cotangent, 'tensor', axis=0, tiled=True)  30.1 us
    all_gather x1, waiting for transfers between devices, shards(): x = lax.all_gather(tokens, 'tensor', axis=0, tiled=True)  27.6 us
    psum x1, blocking collectives, shards(): small = lax.psum((dbe, dbq), 'dp')  23.4 us
  transfers between devices with their start and end apart: 5, of which 5 were waited for; matrix products, arithmetic and copies ran while one was open for 3% of the time, Pallas kernels for 0%

profile of v1, /device:TPU:0, one launch (start us, length us, event | category | flops | bytes accessed | tf_op | source)
XLA Modules:
  0.0 425.6 jit_solution(15924652884632795716)
XLA Ops:
  7.3 0.7 all-gather.3.cloned.1.call-update
  8.0 0.7 all-gather.5.cloned.1.call-update
  8.8 0.9 reshape.95.qkv_b
  13.3 27.6 %all-gather.3.cloned.1.call-done.x_ref = bf16[2048,768]{1,0:T(8,128)(2,1)} async-done(((bf16[512,768]{1,0:T(8,128)(2,1)}), bf16[2048,768]{1,0:T(8,128)(2,1)}) %all-gather.3.cloned.1.call-update) | async-done | bytes 3145744 | tf_op jit(solution)/shard_map/all_gather | solution.py:257
  40.9 30.1 %all-gather.5.cloned.1.call-done.g_ref = bf16[2048,768]{1,0:T(8,128)(2,1)} async-done(((bf16[512,768]{1,0:T(8,128)(2,1)}), bf16[2048,768]{1,0:T(8,128)(2,1)}) %all-gather.5.cloned.1.call-update) | async-done | bytes 3145744 | tf_op jit(solution)/shard_map/all_gather | solution.py:258
  71.0 76.2 %core.1 = (bf16[2048,768]{1,0:T(8,128)(2,1)}, bf16[2048,768]{1,0:T(8,128)(2,1)}, f32[576,768]{1,0:T(8,128)}, f32[192,768]{1,0:T(8,128)}, f32[768,768]{1,0:T(8,12...) custom-call(bf16[2048,768]{1,0:T(8,128)(2,1)} %all-gather.3.cloned.1.call-done.x_ref, ...), custom_call_target="tpu_custom_call" | custom-call | tf_op jit(solution)/shard_map/core/pallas_call | solution.py:264
  147.2 2.9 convert_element_type.47
  150.2 1.1 convert_element_type.49
  151.3 0.8 copy-done.4
  152.1 1.0 convert_element_type.44
  153.1 0.7 convert_element_type.45
  155.0 0.6 copy-done
  156.9 23.4 %all-reduce = (f32[3,192]{1,0:T(4,128)}, f32[768]{0:T(1024)}) all-reduce(f32[3,192]{1,0:T(4,128)S(1)} %reshape.94, f32[768]{0:T(1024)S(1)} %reduce.8), channel_id=1, replica_groups=mesh['dp'=8,'tensor'=4] {'dp'}, use_global_device_ids=true, to_apply=%region_9.0 | all-reduce | flops 1344 | bytes 10752 | tf_op jit(solution)/shard_map/psum | solution.py:328
  180.3 114.7 %all-reduce.4.cloned.1.call-done = (bf16[3,768,192]{1,2,0:T(8,128)(2,1)}, bf16[192,768]{1,0:T(8,128)(2,1)}, bf16[768,768]{1,0:T(8,128)(2,1)}, bf16[768,768]{1,0:T(8,128)(2,1)}) async-done(((bf16[3,768,192]{1,2,0:T(8,128)(2,1)}, bf16[192,768]{1,0:T(8,128)(2,1)}, bf16[768,768]{1,0:T(8,128)(2,1)}, bf16[768,768]{1,0:T(8,128)(2,1)}), (bf16[3,768,192]{1,2,0:T(8,128)(2,1)}, bf16[192,768]{1,0:T(8,128)(2,1)}, ...) | async-done | bytes 3538960 | tf_op jit(solution)/shard_map/psum | solution.py:329
  295.0 2.9 convert_element_type.48
  297.9 1.6 convert_element_type.50
  299.5 1.4 transpose.19
  300.9 0.9 convert_element_type.46
  301.7 32.7 %reduce-scatter.5.cloned.1.call-done = bf16[512,768]{1,0:T(8,128)(2,1)} async-done(((bf16[2048,768]{1,0:T(8,128)(2,1)}), bf16[512,768]{1,0:T(8,128)(2,1)}) %reduce-scatter.5.cloned.1.call-update) | async-done | bytes 786448 | tf_op jit(solution)/shard_map/reduce_scatter | solution.py:316
  334.4 1.9 convert_reduce_fusion
  336.4 38.4 %reduce-scatter.3.cloned.1.call-done = bf16[512,768]{1,0:T(8,128)(2,1)} async-done(((bf16[2048,768]{1,0:T(8,128)(2,1)}), bf16[512,768]{1,0:T(8,128)(2,1)}) %reduce-scatter.3.cloned.1.call-update) | async-done | bytes 786448 | tf_op jit(solution)/shard_map/reduce_scatter | solution.py:315
  374.8 3.4 convert_reduce_fusion.2
  378.3 39.5 %psum.49 = f32[8,768]{1,0:T(8,128)S(1)} all-reduce(f32[8,768]{1,0:T(8,128)S(1)} %scatter.4), channel_id=1, replica_groups=mesh['dp'=8,'tensor'=4] {'dp','tensor'}, use_global_device_ids=true, to_apply=%region_7.0 | all-reduce | flops 6144 | bytes 49152 | tf_op jit(solution)/shard_map/psum | solution.py:327
  417.8 0.6 slice_reduce_fusion
  (64 shorter events, 6.1 us)
Async XLA Ops:
  7.2 1.6 copy-start.12
  7.2 2.5 copy-start.15
  7.2 3.1 copy-start.16
  7.2 3.7 copy-start.17
  7.2 4.3 copy-start.18
  7.2 4.8 %copy-start.19 = (f32[768]{0:T(1024)S(1)}, f32[768]{0:T(1024)}, u32[]{:S(2)}) copy-start(f32[768]{0:T(1024)} %param.29) | copy-start | bytes 9220
  7.2 33.7 %all-gather.3.cloned.1.call-start = ((), (), s32[]{:S(2)}) async-start(), calls=%async_computation.2 | async-start | bytes 3932160 | tf_op jit(solution)/shard_map/all_gather | solution.py:257
  8.0 63.1 %all-gather.5.cloned.1.call-start = ((), (), s32[]{:S(2)}) async-start(), calls=%async_computation.3 | async-start | bytes 3932160 | tf_op jit(solution)/shard_map/all_gather | solution.py:258
  8.7 286.3 %all-reduce.4.cloned.1.call-start = ((), (), s32[]{:S(2)}) async-start(), calls=%async_computation.6 | async-start | bytes 7077888 | tf_op jit(solution)/shard_map/psum | solution.py:329
  147.2 3.0 copy-start.3
  150.2 1.9 copy-start.4
  151.3 1.8 copy-start.7
  153.9 180.6 %reduce-scatter.5.cloned.1.call-start = ((), (), s32[]{:S(2)}) async-start(), calls=%async_computation.5 | async-start | bytes 3932160 | tf_op jit(solution)/shard_map/reduce_scatter | solution.py:316
  154.4 220.4 %reduce-scatter.3.cloned.1.call-start = ((), (), s32[]{:S(2)}) async-start(), calls=%async_computation.4 | async-start | bytes 3932160 | tf_op jit(solution)/shard_map/reduce_scatter | solution.py:315
  154.5 1.1 copy-start
  155.6 1.2 copy-start.20
  295.0 2.9 copy-start.5
  297.9 1.6 copy-start.6
  299.5 1.4 copy-start.8
  300.9 73.9 %copy-start.1 = (bf16[512,768]{1,0:T(8,128)(2,1)S(1)}, bf16[512,768]{1,0:T(8,128)(2,1)}, u32[]{:S(2)}) copy-start(bf16[512,768]{1,0:T(8,128)(2,1)} %param.33) | copy-start | bytes 2359300
  300.9 73.9 %copy-start.13 = (f32[768]{0:T(1024)S(1)}, f32[768]{0:T(1024)}, u32[]{:S(2)}) copy-start(f32[768]{0:T(1024)} %param.31) | copy-start | bytes 9220
  300.9 73.9 %copy-start.14 = (f32[768]{0:T(1024)S(1)}, f32[768]{0:T(1024)}, u32[]{:S(2)}) copy-start(f32[768]{0:T(1024)} %param.27) | copy-start | bytes 9220
  334.4 40.4 %copy-start.2 = (bf16[512,768]{1,0:T(8,128)(2,1)S(1)}, bf16[512,768]{1,0:T(8,128)(2,1)}, u32[]{:S(2)}) copy-start(bf16[512,768]{1,0:T(8,128)(2,1)} %reduce-scatter.5.cloned.1.call-done) | copy-start | bytes 2359300
  374.8 3.4 copy-start.10
  (2 other events, 1.6 us)
Sparse Core Ops, SparseCore 0:
  9.6 31.2 all-gather.2
  42.5 28.5 all-gather.4
  154.0 140.9 all-reduce.3
  297.5 36.8 reduce-scatter.4
  336.8 37.9 reduce-scatter.2

commit v2 on v1

v2 whole, which is shorter than its diff:
```python
import functools

import jax
import jax.numpy as jnp
import numpy as np
from jax import lax
from jax.experimental import pallas as pl
from jax.experimental.pallas import tpu as pltpu
from jax.sharding import PartitionSpec as P

HD = 64
ROT = 16
LEN = 2048
EPS = 1e-05
MASKED = -1e30
F32 = jnp.float32
BF16 = jnp.bfloat16


def dot(a, b, ca, cb):
    return lax.dot_general(a, b, (((ca,), (cb,)), ((), ())), preferred_element_type=F32)


def angle_rows(count):
    half = ROT // 2
    freqs = np.float32(10000.0) ** (
        np.float32(-2.0) * np.arange(half, dtype=np.float32) / np.float32(ROT)
    )
    place = (np.arange(count) % LEN).astype(np.float32)
    angle = (freqs[:, None] * place[None, :]).astype(np.float32)
    return np.cos(angle), np.sin(angle)


def unit_rows(rows):
    values = rows.astype(F32)
    centred = values - jnp.mean(values, -1, keepdims=True)
    inverse = lax.rsqrt(jnp.mean(centred * centred, -1, keepdims=True) + EPS)
    return centred * inverse, inverse

MESH = pl.DeviceIdType.MESH
PARTS = 3


def flip(value, bits):
    bit = 1
    while bit <= bits:
        if (bits // bit) % 2:
            value = value + bit * (1 - 2 * ((value // bit) % 2))
        bit *= 2
    return value


def core(
    n,
    tok,
    cot,
    len_ref,
    par,
    qkv,
    qkv_b,
    wd,
    we,
    wc,
    cos_t,
    sin_t,
    mixed_o,
    gtok_o,
    res_o,
    vec_o,
    x_s,
    g_s,
    n1_s,
    s_s,
    wt,
    qb_s,
    acc,
    res,
    hold,
    qa,
    kt,
    kr,
    va,
    vr,
    dot_s,
    sc,
    pt,
    dkt,
    dvt,
    ctx_s,
    gp,
    dq_s,
    vec,
    vec_in,
    sx,
    rx,
    sz,
    rz,
    ag_send,
    ag_recv,
    rs_send,
    rs_recv,
    x_send,
    x_recv,
    z_send,
    z_recv,
    v_send,
    v_recv,
    out_sem,
    free_sem,
):
    blk, width = tok.shape
    total = x_s.shape[0]
    local = wd.shape[0]
    heads = local // HD
    count = total // blk
    per = LEN // blk
    root = HD**-0.5
    members = n // 2
    piece = acc.shape[1] // members
    dp = lax.axis_index("dp")
    t = lax.axis_index("tensor")
    core_bit = t % 2
    chip_bit = t // 2
    sib = (dp, flip(t, 1))
    across = (dp, flip(t, 2))
    near = (flip(dp, 1), t)
    far = [(flip(dp, 2 * j), t) for j in range(1, members)]
    gain1, bias1, gain2, bias2, exp_b, out_b = (par[r : r + 1, :] for r in range(6))

    def send(src, dst, ssem, rsem, where):
        return pltpu.make_async_remote_copy(
            src_ref=src,
            dst_ref=dst,
            send_sem=ssem,
            recv_sem=rsem,
            device_id=where,
            device_id_type=MESH,
        )

    barrier = pltpu.get_barrier_semaphore()
    greeted = [sib, across, near] + far
    for other in greeted:
        pl.semaphore_signal(barrier, inc=1, device_id=other, device_id_type=MESH)
    pl.semaphore_wait(barrier, len(greeted))

    def block(b):
        return pl.ds(pl.multiple_of(b * blk, blk), blk)

    own = block(t)
    other = block(flip(t, 2))
    gather = [
        send(tok, x_s.at[own], ag_send.at[0], ag_recv.at[0], across),
        send(cot, g_s.at[own], ag_send.at[1], ag_recv.at[1], across),
        send(tok, x_s.at[own], ag_send.at[2], ag_recv.at[2], sib),
        send(cot, g_s.at[own], ag_send.at[3], ag_recv.at[3], sib),
        send(x_s.at[other], x_s.at[other], ag_send.at[4], ag_recv.at[4], sib),
        send(g_s.at[other], g_s.at[other], ag_send.at[5], ag_recv.at[5], sib),
    ]
    gather[0].start()
    gather[2].start()
    gather[3].start()

    x_s[own, :] = tok[...]
    g_s[own, :] = cot[...]
    for c in range(3):
        wt[c * local : (c + 1) * local, :] = jnp.transpose(qkv[c])
        column = jnp.transpose(jnp.broadcast_to(qkv_b[c : c + 1, :], (8, local)))
        qb_s[c * local : (c + 1) * local, :] = column[:, :1]
    for ref in (acc, vec, dkt, dvt):
        ref[...] = jnp.zeros_like(ref)
    one_row = (lax.broadcasted_iota(jnp.int32, (heads, HD, total), 1) == 0).astype(F32)
    qa[:, HD:, :] = one_row.astype(BF16)
    va[:, HD:, :] = one_row[:, : va.shape[1] - HD, :].astype(BF16)

    def forward(b, slot, before_mix):
        rows = block(b)
        unit, _ = unit_rows(x_s[rows, :])
        n1 = (unit * gain1 + bias1).astype(BF16)
        n2 = (unit * gain2 + bias2).astype(BF16)
        n1_s[rows, :] = n1
        hold[2 + slot] = n2
        proj = dot(wt[...], n1, 1, 1) + qb_s[...]
        cosine = cos_t[:, rows]
        sine = sin_t[:, rows]

        def turn(rows_in):
            a = rows_in[: ROT // 2]
            c = rows_in[ROT // 2 : ROT]
            return jnp.concatenate(
                [a * cosine - c * sine, c * cosine + a * sine, rows_in[ROT:]], 0
            )

        place = lax.broadcasted_iota(jnp.int32, (HD, blk), 1) + (b % per) * blk
        first = lax.broadcasted_iota(jnp.int32, (HD, blk), 0) == 0
        extra = jnp.where(first & (place >= len_ref[0]), MASKED, 0.0)
        for h in range(heads):
            lo = h * HD
            q = turn(proj[lo : lo + HD])
            k = turn(proj[local + lo : local + lo + HD])
            v = proj[2 * local + lo : 2 * local + lo + HD]
            qa[h, :HD, rows] = (q * root).astype(BF16)
            kt[h, :, rows] = k.astype(BF16)
            kr[h, rows, :] = jnp.transpose(jnp.concatenate([k, extra], 0)).astype(BF16)
            va[h, :HD, rows] = v.astype(BF16)
            vr[h, rows, :] = jnp.transpose(v).astype(BF16)
        pre = dot(n2, we[...], 1, 0) + exp_b
        big = 0.5 * (1.0 + lax.erf(pre * np.float32(0.5**0.5)))
        act = (pre * big).astype(BF16)
        slope = big + pre * (jnp.exp(-0.5 * pre * pre) * np.float32((2 * np.pi) ** -0.5))
        hold[slot] = act
        hold[4 + slot] = slope.astype(BF16)
        mix = dot(act, wc[...], 1, 0).astype(BF16)
        before_mix()
        x_s[rows, :] = mix

    def backward(b, slot):
        rows = block(b)
        g = g_s[rows, :]
        act = hold[slot]
        n2 = hold[2 + slot]
        grad_ctx = dot(wd[...], g, 1, 1).astype(BF16)
        for h in range(heads):
            dot_s[h, :, rows] = grad_ctx[h * HD : (h + 1) * HD]
        acc[0] += dot(act, g, 0, 0)
        grad_pre = (dot(g, wc[...], 1, 1) * hold[4 + slot].astype(F32)).astype(BF16)
        vec[5:6, :] += jnp.sum(grad_pre.astype(F32), 0, keepdims=True)
        acc[1] += dot(n2, grad_pre, 0, 0)
        part = dot(grad_pre, we[...], 1, 1)
        s_s[rows, :] = (part * gain2).astype(BF16)
        vec[2:3, :] += jnp.sum(part * n2.astype(F32), 0, keepdims=True)
        vec[3:4, :] += jnp.sum(part, 0, keepdims=True)

    def mate(k):
        low = (t + k) % 2
        high = (t // 2 + k // 2) % 2
        return low + 2 * high

    def phase(it, _):
        @pl.when(it == 1)
        def _():
            gather[2].wait_recv()
            gather[3].wait_recv()

        @pl.when(it == 2)
        def _():
            gather[0].wait_send()
            gather[1].start()
            gather[0].wait_recv()
            gather[4].start()

        @pl.when(it == 3)
        def _():
            gather[4].wait_recv()

        @pl.when(it < 4)
        def _():
            def settle():
                @pl.when(it == 2)
                def _():
                    gather[4].wait_send()

            forward(mate(it), it // 3, settle)

        @pl.when(it == 3)
        def _():
            gather[1].wait_recv()
            gather[5].start()

        @pl.when(it == 4)
        def _():
            gather[5].wait_recv()

        @pl.when(it != 2)
        def _():
            backward(mate(it - it // 3), it // 4)

        return 0

    lax.fori_loop(0, 5, phase, 0)
    for k in (1, 2, 3, 5):
        gather[k].wait_send()
    pl.semaphore_signal(free_sem.at[0], inc=1, device_id=sib, device_id_type=MESH)
    pl.semaphore_signal(free_sem.at[1], inc=1, device_id=across, device_id_type=MESH)
    vec[4:5, :] = jnp.sum(cot[...].astype(F32), 0, keepdims=True)

    near_bit = dp % 2
    seat = dp // 2
    ROWS = acc.shape[1]
    LAST = 3 * PARTS

    def lanes(k, bit):
        return pl.ds(pl.multiple_of((k % PARTS) * 256 + bit * 128, 128), 128)

    def band(member):
        return pl.ds(pl.multiple_of(member * piece, piece), piece)

    def seat_of(j):
        return flip(seat, j)

    def halves(k):
        return send(sx, rx.at[k % 2], x_send.at[0], x_recv.at[0, k % 2], near)

    def spread(k):
        return [
            send(
                sz.at[band(seat_of(j))],
                rz.at[k % 2, j - 1],
                z_send.at[0, j - 1],
                z_recv.at[0, k % 2, j - 1],
                far[j - 1],
            )
            for j in range(1, members)
        ]

    def collect(k):
        mine = res.at[k // PARTS, band(seat), lanes(k, near_bit)]
        return [
            send(mine, mine, z_send.at[1, j - 1], z_recv.at[1, k % 2, j - 1], far[j - 1])
            for j in range(1, members)
        ]

    def whole(k):
        half = res.at[k // PARTS, :, lanes(k, near_bit)]
        return send(half, half, x_send.at[1], x_recv.at[1, k % 2], near)

    def beat(b):
        def stage(lag, body):
            k = b - lag
            pl.when((k >= 0) & (k < LAST))(functools.partial(body, k))

        def last(k):
            whole(k).wait()

        def third(k):
            for copy in collect(k):
                copy.wait()
            whole(k).start()

        def second(k):
            for copy in spread(k):
                copy.wait()
            mine = acc[k // PARTS, band(seat), lanes(k, near_bit)]
            for j in range(1, members):
                mine += rz[k % 2, j - 1].astype(F32)
            res[k // PARTS, band(seat), lanes(k, near_bit)] = mine.astype(BF16)
            for copy in collect(k):
                copy.start()

        def first(k):
            halves(k).wait()
            mine = acc[k // PARTS, :, lanes(k, near_bit)] + rx[k % 2].astype(F32)
            acc[k // PARTS, :, lanes(k, near_bit)] = mine
            sz[...] = mine.astype(BF16)
            for copy in spread(k):
                copy.start()

        def zeroth(k):
            sx[...] = acc[k // PARTS, :, lanes(k, 1 - near_bit)].astype(BF16)
            halves(k).start()

        stage(4, last)
        stage(3, third)
        stage(2, second)
        stage(1, first)
        stage(0, zeroth)

    def to_sib(i):
        rows = block(i)
        slot = i // 2
        return [
            send(x_s.at[rows], hold.at[2 * slot], rs_send.at[slot, 0], rs_recv.at[slot, 0], sib),
            send(s_s.at[rows], hold.at[2 * slot + 1], rs_send.at[slot, 1], rs_recv.at[slot, 1], sib),
        ]

    def to_owner(i):
        rows = block(i)
        return [
            send(x_s.at[rows], hold.at[4], rs_send.at[2, 0], rs_recv.at[2, 0], across),
            send(s_s.at[rows], hold.at[5], rs_send.at[2, 1], rs_recv.at[2, 1], across),
        ]

    def hand_over(i):
        @pl.when(core_bit != i % 2)
        def _():
            for copy in to_sib(i):
                copy.start()

    def pass_on(i):
        @pl.when(core_bit == i % 2)
        def _():
            for copy in to_sib(i):
                copy.wait_recv()

        @pl.when((core_bit == i % 2) & (chip_bit != i // 2))
        def _():
            rows = block(i)
            slot = i // 2
            for w, ref in enumerate((x_s, s_s)):
                both = ref[rows, :].astype(F32) + hold[2 * slot + w].astype(F32)
                ref[rows, :] = both.astype(BF16)
            for copy in to_owner(i):
                copy.start()

    beat(0)
    key_i = lax.broadcasted_iota(jnp.int32, (blk, blk), 0)
    query_i = lax.broadcasted_iota(jnp.int32, (blk, blk), 1)

    def attend(step, _):
        i = count - 1 - step
        base = (i // per) * per
        mine = block(i)

        def head(h, _):
            q_aug = qa[h, :, mine]

            def score(j, high):
                s = dot(kr[h, block(j), :], q_aug, 1, 0)
                sc[block(j - base), :] = s
                return jnp.maximum(high, jnp.max(s.reshape(blk // 8, 8, blk), 0))

            high = lax.fori_loop(base, i, score, jnp.full((8, blk), MASKED, F32))
            s = dot(kr[h, mine, :], q_aug, 1, 0)
            s = jnp.where(key_i <= query_i, s, MASKED)
            sc[block(i - base), :] = s
            high = jnp.maximum(high, jnp.max(s.reshape(blk // 8, 8, blk), 0))
            high = jnp.max(high, 0, keepdims=True)

            def weigh(j, out):
                p = jnp.exp(sc[block(j - base), :] - high).astype(BF16)
                pt[block(j - base), :] = p
                return out + dot(va[h, :, block(j)], p, 1, 0)

            out = lax.fori_loop(base, i + 1, weigh, jnp.zeros((va.shape[1], blk), F32))
            scale = 1.0 / out[HD : HD + 1]
            ctx = out[:HD] * scale
            ctx_s[h] = ctx.astype(BF16)
            go = (dot_s[h, :, mine].astype(F32) * scale).astype(BF16)
            inner = jnp.sum(ctx * go.astype(F32), 0, keepdims=True)
            q = q_aug[:HD]

            def back(j, dq):
                cols = block(j)
                p = pt[block(j - base), :]
                dvt[h, :, cols] += dot(go, p, 1, 1)
                dp_t = dot(vr[h, cols, :], go, 1, 0)
                ds = (p.astype(F32) * (dp_t - inner)).astype(BF16)
                dkt[h, :, cols] += dot(q, ds, 1, 1)
                return dq + dot(kt[h, :, cols], ds, 1, 0)

            dq_s[h] = lax.fori_loop(base, i + 1, back, jnp.zeros((HD, blk), F32))

            @pl.when((h == 0) & (step > 0))
            def _():
                pass_on(i + 1)

            tick = step * heads + h
            number = (
                1 * (tick == 0).astype(jnp.int32)
                + 2 * (tick == 1).astype(jnp.int32)
                + 3 * (tick == 2).astype(jnp.int32)
                + 4 * (tick == 4).astype(jnp.int32)
                + 5 * (tick == 6).astype(jnp.int32)
            )

            @pl.when(number > 0)
            def _():
                beat(number)

            return 0

        lax.fori_loop(0, heads, head, 0)
        cosine = cos_t[:, mine]
        sine = sin_t[:, mine]

        def unturn(rows_in):
            a = rows_in[: ROT // 2]
            c = rows_in[ROT // 2 : ROT]
            return jnp.concatenate(
                [a * cosine + c * sine, c * cosine - a * sine, rows_in[ROT:]], 0
            )

        for h in range(heads):
            lo = h * HD
            gp[lo : lo + HD, :] = unturn(dq_s[h] * root).astype(BF16)
            gp[local + lo : local + lo + HD, :] = unturn(dkt[h, :, mine]).astype(BF16)
            gp[2 * local + lo : 2 * local + lo + HD, :] = dvt[h, :, mine].astype(BF16)
        grad_proj = gp[...]
        ctx_all = ctx_s[...].reshape(local, blk)
        mix = dot(ctx_all, wd[...], 0, 0) + x_s[mine, :].astype(F32)
        x_s[mine, :] = mix.astype(BF16)
        part = dot(grad_proj, wt[...], 0, 0) * gain1 + s_s[mine, :].astype(F32)
        s_s[mine, :] = part.astype(BF16)

        @pl.when(step == 0)
        def _():
            pl.semaphore_wait(free_sem.at[0], 1)
            pl.semaphore_wait(free_sem.at[1], 1)

        hand_over(i)
        acc[2, 3 * local :, :] += dot(ctx_all, g_s[mine, :], 1, 0)
        acc[2, : 3 * local, :] += dot(grad_proj, n1_s[mine, :], 1, 0)
        ones = jnp.ones((8, blk), BF16)
        vec[6:7, : 3 * local] += dot(ones, grad_proj, 1, 1)[:1]
        return 0

    lax.fori_loop(0, count, attend, 0)
    w32 = wt[...].astype(F32)
    column = jnp.transpose(jnp.broadcast_to(vec[6:7, : 3 * local], (8, 3 * local)))[:, :1]
    grad_bias = jnp.sum(w32 * column, 0, keepdims=True)
    grad_gain = jnp.sum(w32 * acc[2, : 3 * local, :], 0, keepdims=True)
    vec[1:2, :] = grad_bias
    vec[0:1, :] = (grad_gain - bias1 * grad_bias) / gain1
    vec[2:3, :] = (vec[2:3, :] - bias2 * vec[3:4, :]) / gain2

    swaps = []
    bit = 1
    while bit < n:
        swaps.append((flip(dp, bit), t))
        bit *= 2
    inside = len(swaps)
    swaps += [sib, across]

    def swap(q):
        return send(vec, vec_in.at[q], v_send.at[q], v_recv.at[q], swaps[q])

    shared = lax.broadcasted_iota(jnp.int32, vec.shape, 0) < 5

    def finish_swap(q):
        swap(q).wait()
        extra = vec_in[q]
        if q >= inside:
            extra = jnp.where(shared, extra, 0.0)
        vec[...] += extra

    beat(2 * PARTS)
    swap(0).start()
    pass_on(0)
    steps = max(LAST + 4, 2 * PARTS + len(swaps) + 1)

    def tail(b, _):
        beat(b)
        for q in range(1, len(swaps) + 1):

            @pl.when(b == 2 * PARTS + q)
            def _(q=q):
                finish_swap(q - 1)
                if q < len(swaps):
                    swap(q).start()

        return 0

    lax.fori_loop(2 * PARTS + 1, steps, tail, 0)
    out_copy = pltpu.make_async_copy(res, res_o, out_sem.at[0])
    out_copy.start()
    vec_o[...] = vec[...]

    for copy in to_owner(flip(t, 2)):
        copy.wait()
    slot = chip_bit
    mix = tok[...].astype(F32) + out_b
    s = s_s[own, :].astype(F32)
    mix += x_s[own, :].astype(F32)
    for w in (2 * slot, 4):
        mix += hold[w].astype(F32)
        s += hold[w + 1].astype(F32)
    mixed_o[...] = mix.astype(BF16)
    unit, inverse = unit_rows(tok[...])
    gtok_o[...] = cot[...].astype(F32) + inverse * (
        s - jnp.mean(s, -1, keepdims=True) - unit * jnp.mean(s * unit, -1, keepdims=True)
    )
    for i in range(count):

        @pl.when(core_bit != i % 2)
        def _(i=i):
            for copy in to_sib(i):
                copy.wait_send()

    out_copy.wait()


def shards(
    n,
    tokens,
    input_gain,
    input_bias,
    post_gain,
    post_bias,
    query_key_value,
    query_key_value_bias,
    dense_weight,
    dense_bias,
    expand_weight,
    expand_bias,
    contract_weight,
    contract_bias,
    lengths,
    cotangent,
):
    blk, width = tokens.shape
    local = query_key_value.shape[2]
    heads = local // HD
    total = 4 * blk
    members = n // 2
    swaps = n.bit_length() + 1
    cosine, sine = angle_rows(total)
    par = jnp.stack(
        [
            input_gain,
            input_bias,
            post_gain,
            post_bias,
            expand_bias,
            dense_bias + contract_bias,
        ]
    )
    vmem = pl.BlockSpec(memory_space=pltpu.VMEM)
    smem = pl.BlockSpec(memory_space=pltpu.SMEM)
    dma = pltpu.SemaphoreType.DMA
    mixed, grad_tokens, res, vec = pl.pallas_call(
        functools.partial(core, n),
        name="core",
        out_shape=(
            jax.ShapeDtypeStruct((blk, width), BF16),
            jax.ShapeDtypeStruct((blk, width), F32),
            jax.ShapeDtypeStruct((3, width, width), BF16),
            jax.ShapeDtypeStruct((8, width), F32),
        ),
        in_specs=[vmem, vmem, smem] + [vmem] * 8,
        out_specs=[vmem, vmem, pl.BlockSpec(memory_space=pl.ANY), vmem],
        scratch_shapes=[
            pltpu.VMEM((total, width), BF16),
            pltpu.VMEM((total, width), BF16),
            pltpu.VMEM((total, width), BF16),
            pltpu.VMEM((total, width), BF16),
            pltpu.VMEM((3 * local, width), BF16),
            pltpu.VMEM((3 * local, 1), F32),
            pltpu.VMEM((3, width, width), F32),
            pltpu.VMEM((3, width, width), BF16),
            pltpu.VMEM((6, blk, width), BF16),
            pltpu.VMEM((heads, 2 * HD, total), BF16),
            pltpu.VMEM((heads, HD, total), BF16),
            pltpu.VMEM((heads, total, 2 * HD), BF16),
            pltpu.VMEM((heads, HD + 16, total), BF16),
            pltpu.VMEM((heads, total, HD), BF16),
            pltpu.VMEM((heads, HD, total), BF16),
            pltpu.VMEM((LEN, blk), F32),
            pltpu.VMEM((LEN, blk), BF16),
            pltpu.VMEM((heads, HD, total), F32),
            pltpu.VMEM((heads, HD, total), F32),
            pltpu.VMEM((heads, HD, blk), BF16),
            pltpu.VMEM((3 * local, blk), BF16),
            pltpu.VMEM((heads, HD, blk), F32),
            pltpu.VMEM((8, width), F32),
            pltpu.VMEM((swaps, 8, width), F32),
            pltpu.VMEM((width, 128), BF16),
            pltpu.VMEM((2, width, 128), BF16),
            pltpu.VMEM((width, 128), BF16),
            pltpu.VMEM((2, members - 1, width // members, 128), BF16),
            dma((6,)),
            dma((6,)),
            dma((3, 2)),
            dma((3, 2)),
            dma((2,)),
            dma((2, 2)),
            dma((2, members - 1)),
            dma((2, 2, members - 1)),
            dma((swaps,)),
            dma((swaps,)),
            dma((1,)),
            pltpu.SemaphoreType.REGULAR((2,)),
        ],
        compiler_params=pltpu.CompilerParams(
            vmem_limit_bytes=63 * 2**20, collective_id=0, has_side_effects=True
        ),
    )(
        tokens,
        cotangent,
        lengths,
        par,
        query_key_value,
        query_key_value_bias,
        dense_weight,
        expand_weight,
        contract_weight,
        cosine,
        sine,
    )
    rest = 3 * local
    grad_qkv = jnp.transpose(res[2, :rest].reshape(3, local, width), (0, 2, 1)).astype(F32)
    return (
        mixed,
        grad_tokens,
        vec[0],
        vec[1],
        vec[2],
        vec[3],
        grad_qkv,
        vec[6, :rest].reshape(3, local),
        res[2, rest:].astype(F32),
        vec[4],
        res[1].astype(F32),
        vec[5],
        res[0].astype(F32),
        vec[4],
    )


def solution(mesh):
    rows = P(("dp", "tensor"), None)
    weights = (
        P(None, None, "tensor"),
        P(None, "tensor"),
        P("tensor", None),
        P(),
        P(None, "tensor"),
        P("tensor"),
        P("tensor", None),
        P(),
    )
    return jax.shard_map(
        functools.partial(shards, mesh.shape["dp"]),
        mesh=mesh,
        in_specs=(rows, P(), P(), P(), P()) + weights + (P("dp"), rows),
        out_specs=(rows, rows, P(), P(), P(), P()) + weights,
        check_vma=False,
    )
```

time: 426 us -> 184 us (0.43)
  waiting for transfers between devices: 246 us -> 0 us
  Pallas kernels: 76.2 us -> 164 us
  blocking collectives: 62.9 us -> 0 us
  between operations: 14.6 us -> 1.32 us
  other arithmetic: 18.6 us -> 5.45 us
  local copies, waits for them, and re-layouts: 7.08 us -> 13.4 us
    psum x1 -> x0, waiting for transfers between devices: 115 us -> none  [shards(): lax.psum((dwt.astype(BF16), dwd.astype(BF16), dwe.astype(BF16), dwc.astyp...]
    pallas_call x1, Pallas kernels: 76.2 us -> 164 us  [shards(): pl.pallas_call(functools.partial(core, n), name='core', out_shape=(jax.Sh...]
    reduce_scatter x2 -> x0, waiting for transfers between devices: 71.1 us -> none  [the longest x1 38.4 us: shards(): mix = lax.psum_scatter(mix_p, 'tensor', scatter_dimension=0, tiled=True)]
    psum x2 -> x0, blocking collectives: 62.9 us -> none  [the longest x1 39.5 us: shards(): vec = lax.psum(vec, ('dp', 'tensor'))]
    all_gather x2 -> x0, waiting for transfers between devices: 57.7 us -> none  [the longest x1 30.1 us: shards(): g = lax.all_gather(cotangent, 'tensor', axis=0, tiled=True)]
    convert_element_type x7 -> x3, other arithmetic: 11.2 us -> 4.75 us  [the longest x1 2.54 us: shards(): res[0].astype(F32)]
    reduce_sum x4 -> x0, other arithmetic: 5.84 us -> none  [the longest x1 3.37 us: shards(): vec = vec.at[4].set(jnp.sum(cotangent.astype(F32), 0))]
    another operation x1 -> x8, local copies, waits for them, and re-layouts: 0.01 us -> 4.76 us  [the longest x7 4.09 us: shards(): jnp.stack([input_gain, input_bias, post_gain, post_bias, expand_bias, den...]
  transfers between devices with their start and end apart: 5 -> 0, of which waited for: 5 -> 0; matrix products, arithmetic and copies ran while one was open for 3% -> 0% of each run, Pallas kernels for 0% -> 0%
where the time goes in v2:
time: 184 us
  Pallas kernels  164 us (89%)
  local copies, waits for them, and re-layouts  13.4 us (7%)
  other arithmetic  5.45 us (3%)
    pallas_call x1, Pallas kernels, shards(): pl.pallas_call(functools.partial(core, n), name='core', out_shape=(jax.Sh...  164 us
    unnamed x12, local copies, waits for them, and re-layouts  4.95 us
    another operation x7, local copies, waits for them, and re-layouts, shards(): jnp.stack([input_gain, input_bias, post_gain, post_bias, expand_bias, den...  4.09 us

profile of v2, /device:TPU:0, one launch (start us, length us, event | category | flops | bytes accessed | tf_op | source)
XLA Modules:
  0.0 183.8 jit_solution(18010694352432505088)
XLA Ops:
  1.3 0.7 stack.21
  2.0 0.7 stack.22
  2.7 0.7 stack.23
  3.4 0.7 stack.24
  4.1 0.7 stack.25
  4.7 0.7 add.3
  5.5 0.6 stack.27.par
  6.1 2.3 %copy.31.qkv = bf16[3,768,192]{2,1,0:T(8,128)(2,1)} copy(bf16[3,768,192]{1,2,0:T(8,128)(2,1)} %param.22) | data formatting | bytes 1769472 | tf_op args[5]
  8.4 163.6 %core.1 = (bf16[512,768]{1,0:T(8,128)(2,1)}, f32[512,768]{1,0:T(8,128)}, bf16[3,768,768]{2,1,0:T(8,128)(2,1)}, f32[8,768]{1,0:T(8,128)}) custom-call(bf16[512,768]{1,0:T(8,128)(2,1)} %tok.1, bf16[512,768]{1,0:T(8,128)(2,1)} %cot.1, s32[1]{0:T(128)S(6)} %copy.35.len_ref, f32[6,768]{1,0:T(8,128)} %stack.27.par, bf16[3,768,192]{2,1,0:T(8,128)(2,1)} %copy.31.qkv, ...), custom_call_target="tpu_custom_call" | custom-call | tf_op jit(solution)/shard_map/core/pallas_call | solution.py:619
  172.0 1.6 slice_reduce_fusion
  173.7 0.0 copy-start.3
  173.7 1.4 slice.38
  175.0 1.4 convert_bitcast_fusion
  176.4 0.7 slice_reduce_fusion.6
  177.1 0.7 reshape_squeeze.4
  177.8 0.0 copy-done
  177.8 0.9 bitcast_convert_fusion.2
  178.7 2.5 %bitcast_convert_fusion = (f32[768,768]{1,0:T(8,128)}, f32[768,768]{1,0:T(8,128)}) fusion(bf16[3,768,768]{2,1,0:T(8,128)(2,1)S(1)} %copy-done), kind=kLoop, calls=%fused_computation.1 | loop fusion | flops 1179648 | bytes 7077888 | tf_op jit(solution)/shard_map/convert_element_type | solution.py:703
  181.2 0.0 copy-done.3
  181.2 0.6 copy.36
  181.8 0.0 copy-done.2
  181.8 0.9 copy.37
  182.7 0.0 copy-done.1
  182.7 1.1 copy.38
  (4 shorter events, 0.0 us)
Async XLA Ops:
  173.7 7.6 %copy-start.3 = (f32[768]{0:T(1024)}, f32[768]{0:T(1024)S(1)}, u32[]{:S(2)}) copy-start(f32[768]{0:T(1024)S(1)} %get-tuple-element.81) | copy-start | bytes 9220
  173.7 4.1 %copy-start = (bf16[3,768,768]{2,1,0:T(8,128)(2,1)S(1)}, bf16[3,768,768]{2,1,0:T(8,128)(2,1)}, u32[]{:S(2)}) copy-start(bf16[3,768,768]{2,1,0:T(8,128)(2,1)} %get-tuple-element.21) | copy-start | bytes 10616836
  178.7 3.1 %copy-start.2 = (bf16[512,768]{1,0:T(8,128)(2,1)S(1)}, bf16[512,768]{1,0:T(8,128)(2,1)}, u32[]{:S(2)}) copy-start(bf16[512,768]{1,0:T(8,128)(2,1)} %get-tuple-element.72) | copy-start | bytes 2359300
  181.2 1.5 copy-start.1

commit v3 on v2

v3 whole, which is shorter than its diff:
```python
import functools

import jax
import jax.numpy as jnp
import numpy as np
from jax import lax
from jax.experimental import pallas as pl
from jax.experimental.pallas import tpu as pltpu
from jax.sharding import PartitionSpec as P

HD = 64
ROT = 16
LEN = 2048
EPS = 1e-05
MASKED = -1e30
F32 = jnp.float32
BF16 = jnp.bfloat16


def dot(a, b, ca, cb):
    return lax.dot_general(a, b, (((ca,), (cb,)), ((), ())), preferred_element_type=F32)


def angle_rows(count):
    half = ROT // 2
    freqs = np.float32(10000.0) ** (
        np.float32(-2.0) * np.arange(half, dtype=np.float32) / np.float32(ROT)
    )
    place = (np.arange(count) % LEN).astype(np.float32)
    angle = (freqs[:, None] * place[None, :]).astype(np.float32)
    return np.cos(angle), np.sin(angle)


def unit_rows(rows):
    values = rows.astype(F32)
    centred = values - jnp.mean(values, -1, keepdims=True)
    inverse = lax.rsqrt(jnp.mean(centred * centred, -1, keepdims=True) + EPS)
    return centred * inverse, inverse

MESH = pl.DeviceIdType.MESH
SUB = 256
UNIT = 1.25


def flip(value, bits):
    bit = 1
    while bit <= bits:
        if (bits // bit) % 2:
            value = value + bit * (1 - 2 * ((value // bit) % 2))
        bit *= 2
    return value


def pieces(n):
    made = [(SUB * k, SUB, k, 0) for k in range(7)]
    parts = 2 if n <= 16 else 1
    size = SUB // parts
    for k in range(2 * parts):
        made.append((7 * SUB + size * k, size, k // parts, size * (k % parts)))
    return made


def plan(rounds, chunks, points, width, margin=0.4, rate=0.05, delay=2.6, work=0.35):
    free = [points[0], points[0]]
    clock = points[0]
    reached = 0
    todo = [(when, k, 0) for k, (when, _) in enumerate(chunks)]
    made = []
    while todo:
        todo.sort()
        when, k, step = todo.pop(0)
        later = [(at, u) for u, at in enumerate(points) if at >= when and u >= reached]
        if later:
            at, reached = later[0]
            u = reached
            clock = max(at, clock)
        else:
            u = reached = len(points)
            clock = max(when, clock, points[-1] + 1.5)
        clock += work
        made.append((clock, u, k, step))
        if step < 2 * rounds + 2:
            size = chunks[k][1] * width * 1e-6
            turn = min(step, 2 * rounds + 1 - step)
            kind = 1 if turn else 0
            free[kind] = max(free[kind], clock) + size / 2**turn / rate
            todo.append((free[kind] + delay + (margin if later else 0.0), k, step + 1))
    return made


def core(
    n,
    tok,
    cot,
    len_ref,
    gain1_r,
    bias1_r,
    gain2_r,
    bias2_r,
    exp_r,
    outb1_r,
    outb2_r,
    qkv,
    qkv_b,
    wd_h,
    we_h,
    wc_h,
    cos_t,
    sin_t,
    mixed_o,
    gtok_o,
    res_o,
    vec_o,
    x_s,
    g_s,
    n1_s,
    s_s,
    wt,
    wd,
    we,
    wc,
    qb_s,
    acc,
    res,
    hold,
    qa,
    kt,
    kr,
    va,
    vr,
    dot_s,
    pt,
    mrun,
    dkt,
    dvt,
    ctx_s,
    dq_s,
    vec,
    vec_in,
    sx,
    rx,
    rz,
    in_sem,
    ag_send,
    ag_recv,
    rs_send,
    rs_recv,
    ar_send,
    ar_recv,
    v_send,
    v_recv,
    out_sem,
    free_sem,
):
    blk, width = tok.shape
    total = x_s.shape[0]
    local = wd.shape[0]
    heads = local // HD
    count = total // blk
    per = LEN // blk
    root = HD**-0.5
    band = 4 * HD
    attn = 2 * width
    rounds = n.bit_length() - 2
    dp = lax.axis_index("dp")
    t = lax.axis_index("tensor")
    core_bit = t % 2
    chip_bit = t // 2
    sib = (dp, flip(t, 1))
    across = (dp, flip(t, 2))
    peers = [(flip(dp, 2**q), t) for q in range(rounds + 1)]

    def send(src, dst, ssem, rsem, where):
        return pltpu.make_async_remote_copy(
            src_ref=src,
            dst_ref=dst,
            send_sem=ssem,
            recv_sem=rsem,
            device_id=where,
            device_id_type=MESH,
        )

    def block(b):
        return pl.ds(pl.multiple_of(b * blk, blk), blk)

    own = block(t)
    other = block(flip(t, 2))
    fetch = [
        pltpu.make_async_copy(tok, x_s.at[own], in_sem.at[0]),
        pltpu.make_async_copy(cot, g_s.at[own], in_sem.at[1]),
        pltpu.make_async_copy(we_h, we, in_sem.at[2]),
        pltpu.make_async_copy(wc_h, wc, in_sem.at[3]),
        pltpu.make_async_copy(wd_h, wd, in_sem.at[4]),
    ]
    for h in range(heads):
        for c in range(3):
            fetch.append(
                pltpu.make_async_copy(
                    qkv.at[c, h * HD : (h + 1) * HD, :],
                    wt.at[(3 * h + c) * HD : (3 * h + c + 1) * HD, :],
                    in_sem.at[5 + 3 * h + c],
                )
            )
    for copy in fetch:
        copy.start()

    barrier = pltpu.get_barrier_semaphore()
    greeted = [sib, across] + peers
    for who in greeted:
        pl.semaphore_signal(barrier, inc=1, device_id=who, device_id_type=MESH)
    pl.semaphore_wait(barrier, len(greeted))

    gather = [
        send(tok, x_s.at[own], ag_send.at[0], ag_recv.at[0], across),
        send(cot, g_s.at[own], ag_send.at[1], ag_recv.at[1], across),
        send(tok, x_s.at[own], ag_send.at[2], ag_recv.at[2], sib),
        send(cot, g_s.at[own], ag_send.at[3], ag_recv.at[3], sib),
        send(x_s.at[other], x_s.at[other], ag_send.at[4], ag_recv.at[4], sib),
        send(g_s.at[other], g_s.at[other], ag_send.at[5], ag_recv.at[5], sib),
    ]
    gather[0].start()
    gather[2].start()
    gather[3].start()

    gain1, bias1, gain2, bias2, exp_b = (
        r[...].reshape(1, width) for r in (gain1_r, bias1_r, gain2_r, bias2_r, exp_r)
    )
    for c in range(3):
        column = jnp.transpose(jnp.broadcast_to(qkv_b[c : c + 1, :], (8, local)))
        for h in range(heads):
            qb_s[(3 * h + c) * HD : (3 * h + c + 1) * HD, :] = column[h * HD : (h + 1) * HD, :1]
    for ref in (acc, vec, dkt, dvt):
        ref[...] = jnp.zeros_like(ref)
    one_row = (lax.broadcasted_iota(jnp.int32, (heads, HD, total), 1) == 0).astype(F32)
    qa[:, HD:, :] = one_row.astype(BF16)
    va[:, HD:, :] = one_row[:, : va.shape[1] - HD, :].astype(BF16)
    for copy in fetch:
        copy.wait()

    half = width // 2
    near_bit = dp % 2
    seat = dp // 2

    def lanes(bit):
        return pl.ds(pl.multiple_of(bit * half, 128), half)

    my_lanes = lanes(near_bit)
    chunks = pieces(n)

    def first_of(k, q):
        first = 0
        for p in range(q):
            first = first + ((seat // 2**p) % 2) * (chunks[k][1] // 2 ** (p + 1))
        return first

    def span(k, q, first):
        size = chunks[k][1] // 2**q
        return pl.ds(pl.multiple_of(chunks[k][0] + first, chunks[k][1] // 2**rounds), size)

    def kept(k, q):
        return span(k, q, first_of(k, q))

    def given(k, q):
        bit = (seat // 2 ** (q - 1)) % 2
        return span(k, q, first_of(k, q - 1) + (1 - bit) * (chunks[k][1] // 2**q))

    def whole_slot(k):
        _, rows, slot, low = chunks[k]
        return slot, pl.ds(low, rows)

    def slot_part(k, q):
        _, rows, slot, low = chunks[k]
        return slot, pl.ds(low + rows - rows // 2 ** (q - 1), rows // 2**q)

    def ar_copy(k, step):
        sems = (ar_send.at[step, k], ar_recv.at[step, k])
        if step == 0:
            return send(sx.at[whole_slot(k)], rx.at[whole_slot(k)], *sems, peers[0])
        if step <= rounds:
            return send(sx.at[slot_part(k, step)], rz.at[slot_part(k, step)], *sems, peers[step])
        if step <= 2 * rounds:
            q = 2 * rounds - step + 1
            piece = res.at[kept(k, q), my_lanes]
            return send(piece, piece, *sems, peers[q])
        piece = res.at[kept(k, 0), my_lanes]
        return send(piece, piece, *sems, peers[0])

    def advance(k, step):
        if step == 0:
            sx[whole_slot(k)] = acc[kept(k, 0), lanes(1 - near_bit)].astype(BF16)
        else:
            ar_copy(k, step - 1).wait()
        if step == 1:
            mine = kept(k, 0)
            acc[mine, my_lanes] = acc[mine, my_lanes] + rx[whole_slot(k)].astype(F32)
        if 2 <= step <= rounds + 1:
            mine = kept(k, step - 1)
            done = acc[mine, my_lanes] + rz[slot_part(k, step - 1)].astype(F32)
            if step <= rounds:
                acc[mine, my_lanes] = done
            else:
                res[mine, my_lanes] = done.astype(BF16)
        if 1 <= step <= rounds:
            sx[slot_part(k, step)] = acc[given(k, step), my_lanes].astype(BF16)
        if step < 2 * rounds + 2:
            ar_copy(k, step).start()

    clock = -7.0
    points = [-7.0, -5.0, -3.2, -1.6]
    clock = 0.0
    for group in (1, heads - 1):
        for i in range(count - 1, -1, -1):
            for _ in range(group * (i + 1)):
                clock += UNIT
                points.append(clock)
            clock += 0.9 if group == 1 else 2.2
            if group == 1 and i == 0:
                first_head = clock
    last_time = clock
    ready = [points[0]] * 3 + [points[2]] * 3 + [first_head]
    begin = last_time
    while True:
        times = ready + [begin] * (len(chunks) - len(ready))
        made = plan(rounds, [(r, c[1]) for r, c in zip(times, chunks)], points, width)
        through = max(at for at, (_, _, k, step) in enumerate(made) if k < 2)
        if through < min(at for at, (_, _, k, _) in enumerate(made) if k > 6):
            break
        begin = max(begin, made[through][0]) + 0.1
    ticks = {}
    after = []
    for when, u, k, step in made:
        if u < len(points):
            ticks.setdefault(u, []).append((k, step))
        else:
            after.append((when, k, step))

    def forward(b, slot, before_mix):
        rows = block(b)
        unit, _ = unit_rows(x_s[rows, :])
        n1 = (unit * gain1 + bias1).astype(BF16)
        n2 = (unit * gain2 + bias2).astype(BF16)
        n1_s[rows, :] = n1
        hold[2 + slot] = n2
        pre = dot(n2, we[...], 1, 0) + exp_b
        big = 0.5 * (1.0 + lax.erf(pre * np.float32(0.5**0.5)))
        act = (pre * big).astype(BF16)
        slope = big + pre * (jnp.exp(-0.5 * pre * pre) * np.float32((2 * np.pi) ** -0.5))
        hold[slot] = act
        hold[4 + slot] = slope.astype(BF16)
        mix = dot(act, wc[...], 1, 0).astype(BF16)
        before_mix()
        x_s[rows, :] = mix
        proj = dot(wt[...], n1, 1, 1) + qb_s[...]
        cosine = cos_t[:, rows]
        sine = sin_t[:, rows]

        def turn(rows_in):
            a = rows_in[: ROT // 2]
            c = rows_in[ROT // 2 : ROT]
            return jnp.concatenate(
                [a * cosine - c * sine, c * cosine + a * sine, rows_in[ROT:]], 0
            )

        place = lax.broadcasted_iota(jnp.int32, (HD, blk), 1) + (b % per) * blk
        first = lax.broadcasted_iota(jnp.int32, (HD, blk), 0) == 0
        extra = jnp.where(first & (place >= len_ref[0]), MASKED, 0.0)
        for h in range(heads):
            lo = 3 * h * HD
            q = turn(proj[lo : lo + HD])
            k = turn(proj[lo + HD : lo + 2 * HD])
            v = proj[lo + 2 * HD : lo + 3 * HD]
            qa[h, :HD, rows] = (q * root).astype(BF16)
            kt[h, :, rows] = k.astype(BF16)
            kr[h, rows, :] = jnp.transpose(jnp.concatenate([k, extra], 0)).astype(BF16)
            va[h, :HD, rows] = v.astype(BF16)
            vr[h, rows, :] = jnp.transpose(v).astype(BF16)

    def mate(k):
        low = (t + k) % 2
        high = (t // 2 + k // 2) % 2
        return low + 2 * high

    def phase(it, _):
        late = it // 4 > 0
        b = mate(jnp.where(late, 2 + it % 2, it))
        slot = jnp.where(late, it % 2, it // 3)
        rows = block(b)

        @pl.when(it == 1)
        def _():
            gather[2].wait_recv()
            gather[3].wait_recv()

        @pl.when(it == 2)
        def _():
            gather[0].wait_send()
            gather[1].start()
            gather[0].wait_recv()
            gather[4].start()

        @pl.when(it == 3)
        def _():
            gather[4].wait_recv()

        @pl.when(it < 4)
        def _():
            def settle():
                @pl.when(it == 2)
                def _():
                    gather[4].wait_send()

            forward(b, slot, settle)

        @pl.when(it == 4)
        def _():
            gather[1].wait_recv()
            gather[5].start()

        @pl.when(it == 5)
        def _():
            gather[5].wait_recv()

        for u in range(4):

            @pl.when(it == 6 + u)
            def _(u=u):
                for k, at in ticks.get(u, ()):
                    advance(k, at)

        @pl.when((it < 2) | (it == 4) | (it == 5))
        def _():
            acc[:width] += dot(hold[slot], g_s[rows, :], 0, 0)

        @pl.when((it < 2) | (it == 6) | (it == 7))
        def _():
            slope = hold[4 + slot].astype(F32)
            grad_pre = (dot(g_s[rows, :], wc[...], 1, 1) * slope).astype(BF16)
            hold[slot] = grad_pre
            vec[5:6, :] += jnp.sum(grad_pre.astype(F32), 0, keepdims=True)
            acc[width : 2 * width] += dot(hold[2 + slot], grad_pre, 0, 0)

        @pl.when((it < 2) | (it > 7))
        def _():
            part = dot(hold[slot], we[...], 1, 1)
            s_s[rows, :] = (part * gain2).astype(BF16)
            vec[2:3, :] += jnp.sum(part * hold[2 + slot].astype(F32), 0, keepdims=True)
            vec[3:4, :] += jnp.sum(part, 0, keepdims=True)
            grad_ctx = dot(wd[...], g_s[rows, :], 1, 1).astype(BF16)
            for h in range(heads):
                dot_s[h, :, rows] = grad_ctx[h * HD : (h + 1) * HD]

        return 0

    lax.fori_loop(0, 10, phase, 0)
    for k in (1, 2, 3, 5):
        gather[k].wait_send()
    pl.semaphore_signal(free_sem.at[0], inc=1, device_id=sib, device_id_type=MESH)
    pl.semaphore_signal(free_sem.at[1], inc=1, device_id=across, device_id_type=MESH)

    def to_sib(i):
        rows = block(i)
        slot = i // 2
        return [
            send(x_s.at[rows], hold.at[2 * slot], rs_send.at[slot, 0], rs_recv.at[slot, 0], sib),
            send(s_s.at[rows], hold.at[2 * slot + 1], rs_send.at[slot, 1], rs_recv.at[slot, 1], sib),
        ]

    def to_owner(i):
        rows = block(i)
        return [
            send(x_s.at[rows], hold.at[4], rs_send.at[2, 0], rs_recv.at[2, 0], across),
            send(s_s.at[rows], hold.at[5], rs_send.at[2, 1], rs_recv.at[2, 1], across),
        ]

    def hand_over(i):
        @pl.when(core_bit != i % 2)
        def _():
            for copy in to_sib(i):
                copy.start()

    def pass_on(i):
        @pl.when(core_bit == i % 2)
        def _():
            for copy in to_sib(i):
                copy.wait_recv()

        @pl.when((core_bit == i % 2) & (chip_bit != i // 2))
        def _():
            rows = block(i)
            slot = i // 2
            for w, ref in enumerate((x_s, s_s)):
                both = ref[rows, :].astype(F32) + hold[2 * slot + w].astype(F32)
                ref[rows, :] = both.astype(BF16)
            for copy in to_owner(i):
                copy.start()

    key_i = lax.broadcasted_iota(jnp.int32, (blk, blk), 0)
    query_i = lax.broadcasted_iota(jnp.int32, (blk, blk), 1)

    def gain_sum(some):
        for h in some:
            w32 = wt[3 * h * HD : 3 * (h + 1) * HD, :].astype(F32)
            mine = acc[attn + h * band : attn + h * band + 3 * HD, :]
            vec[0:1, :] += jnp.sum(w32 * mine, 0, keepdims=True)

    def attend(visit, _):
        group = visit // count
        step = visit % count
        i = count - 1 - step
        base = (i // per) * per
        mine = block(i)
        size = 1 + group * (heads - 2)
        passed = size * (count * step - (step * (step - 1)) // 2)
        passed += 4 + group * (count * (count + 1) // 2)

        def head(h, _):
            q_aug = qa[h, :, mine]

            def weigh(j, s, high, out):
                top = jnp.max(jnp.max(s.reshape(blk // 8, 8, blk), 0), 0, keepdims=True)
                top = jnp.maximum(high, top)
                p = jnp.exp(s - top).astype(BF16)
                pt[block(j - base), :] = p
                mrun[pl.ds(j - base, 1), :] = top
                return top, out * jnp.exp(high - top) + dot(va[h, :, block(j)], p, 1, 0)

            def onward(j, carry):
                return weigh(j, dot(kr[h, block(j), :], q_aug, 1, 0), *carry)

            begin = (jnp.full((1, blk), MASKED, F32), jnp.zeros((va.shape[1], blk), F32))
            carry = lax.fori_loop(base, i, onward, begin)
            s = dot(kr[h, mine, :], q_aug, 1, 0)
            high, out = weigh(i, jnp.where(key_i <= query_i, s, MASKED), *carry)
            scale = 1.0 / out[HD : HD + 1]
            ctx = out[:HD] * scale
            ctx_s[h, :, mine] = ctx.astype(BF16)
            grad = dot_s[h, :, mine].astype(F32) * scale
            q = q_aug[:HD]

            def back(j, dq):
                cols = block(j)
                p = pt[block(j - base), :]
                go = (grad * jnp.exp(mrun[pl.ds(j - base, 1), :] - high)).astype(BF16)
                inner = jnp.sum(ctx * go.astype(F32), 0, keepdims=True)
                dvt[h, :, cols] += dot(go, p, 1, 1)
                dp_t = dot(vr[h, cols, :], go, 1, 0)
                ds = (p.astype(F32) * (dp_t - inner)).astype(BF16)
                dkt[h, :, cols] += dot(q, ds, 1, 1)
                unit = passed + (h - group) * (i + 1) + (j - base)
                for u, steps in ticks.items():
                    if u < 4:
                        continue

                    @pl.when(unit == u)
                    def _(steps=steps):
                        for k, at in steps:
                            advance(k, at)

                return dq + dot(kt[h, :, cols], ds, 1, 0)

            dq_s[h] = lax.fori_loop(base, i + 1, back, jnp.zeros((HD, blk), F32))

            @pl.when((h == 1) & (step > 0))
            def _():
                pass_on(i + 1)

            return 0

        lax.fori_loop(group, group + size, head, 0)
        cosine = cos_t[:, mine]
        sine = sin_t[:, mine]

        def unturn(rows_in):
            a = rows_in[: ROT // 2]
            c = rows_in[ROT // 2 : ROT]
            return jnp.concatenate(
                [a * cosine + c * sine, c * cosine - a * sine, rows_in[ROT:]], 0
            )

        def projected(some):
            parts = [(qa[h, :HD, mine], kt[h, :, mine], va[h, :HD, mine]) for h in some]
            return jnp.concatenate([x for three in parts for x in three], 0)

        def weights(some):
            for h in some:
                qa[h, :HD, mine] = unturn(dq_s[h] * root).astype(BF16)
                kt[h, :, mine] = unturn(dkt[h, :, mine]).astype(BF16)
                va[h, :HD, mine] = dvt[h, :, mine].astype(BF16)
            lo, hi = some[0], some[-1] + 1
            ctx = ctx_s[lo:hi, :, mine].reshape((hi - lo) * HD, blk)
            grad_proj = projected(some)
            grad_d = dot(ctx, g_s[mine, :], 1, 0)
            grad_w = dot(grad_proj, n1_s[mine, :], 1, 0)
            for h in some:
                at = attn + h * band
                acc[at : at + 3 * HD, :] += grad_w[3 * (h - lo) * HD : 3 * (h - lo + 1) * HD]
                acc[at + 3 * HD : at + band, :] += grad_d[(h - lo) * HD : (h - lo + 1) * HD]

        @pl.when(group == 0)
        def _():
            weights([0])

            @pl.when(step == count - 1)
            def _():
                gain_sum([0])

        @pl.when(group == 1)
        def _():
            weights(list(range(1, heads)))
            ctx = ctx_s[:, :, mine].reshape(local, blk)
            mix = dot(ctx, wd[...], 0, 0) + x_s[mine, :].astype(F32)
            x_s[mine, :] = mix.astype(BF16)
            grad_proj = projected(range(heads))
            part = dot(grad_proj, wt[...], 0, 0) * gain1 + s_s[mine, :].astype(F32)
            s_s[mine, :] = part.astype(BF16)

            @pl.when(step == 0)
            def _():
                pl.semaphore_wait(free_sem.at[0], 1)
                pl.semaphore_wait(free_sem.at[1], 1)

            hand_over(i)
            ones = jnp.ones((8, blk), BF16)
            vec[6:7, : 3 * local] += dot(ones, grad_proj, 1, 1)[:1]

        return 0

    lax.fori_loop(0, 2 * count, attend, 0)
    again = pltpu.make_async_copy(tok, n1_s.at[own], in_sem.at[0])
    again.start()

    swaps = peers + [sib, across]
    inside = len(peers)

    def swap(q):
        return send(vec, vec_in.at[q], v_send.at[q], v_recv.at[q], swaps[q])

    shared = lax.broadcasted_iota(jnp.int32, vec.shape, 0) < 5

    def finish_swap(q):
        swap(q).wait()
        extra = vec_in[q]
        if q >= inside:
            extra = jnp.where(shared, extra, 0.0)
        vec[...] += extra

    def vectors():
        w32 = wt[...].astype(F32)
        column = jnp.transpose(jnp.broadcast_to(vec[6:7, : 3 * local], (8, 3 * local)))[:, :1]
        grad_bias = jnp.sum(w32 * column, 0, keepdims=True)
        gain_sum(range(1, heads))
        vec[1:2, :] = grad_bias
        vec[0:1, :] = (vec[0:1, :] - bias1 * grad_bias) / gain1
        vec[2:3, :] = (vec[2:3, :] - bias2 * vec[3:4, :]) / gain2
        vec[4:5, :] = jnp.sum(g_s[own, :].astype(F32), 0, keepdims=True)

    def tokens_out():
        for copy in to_owner(flip(t, 2)):
            copy.wait()
        again.wait()
        rows = n1_s[own, :]
        mix = rows.astype(F32) + (outb1_r[...] + outb2_r[...]).reshape(1, width)
        mix += x_s[own, :].astype(F32)
        s = s_s[own, :].astype(F32)
        for w in (2 * chip_bit, 4):
            mix += hold[w].astype(F32)
            s += hold[w + 1].astype(F32)
        mixed_o[...] = mix.astype(BF16)
        unit, inverse = unit_rows(rows)
        gtok_o[...] = g_s[own, :].astype(F32) + inverse * (
            s - jnp.mean(s, -1, keepdims=True) - unit * jnp.mean(s * unit, -1, keepdims=True)
        )

    jobs = [(when, functools.partial(advance, k, step)) for when, k, step in after]
    jobs.append((last_time + 2.9, vectors))
    jobs.append((last_time + 3.0, functools.partial(pass_on, 0)))
    for q in range(len(swaps)):

        def trade(q=q):
            if q > 0:
                finish_swap(q - 1)
            swap(q).start()

        jobs.append((last_time + 4.0 + 3.5 * q, trade))
    jobs.append((last_time + 4.0 + 3.5 * len(swaps), lambda: finish_swap(len(swaps) - 1)))
    jobs.append((last_time + 32.0, tokens_out))
    for _, job in sorted(jobs, key=lambda pair: pair[0]):
        job()
    out_copy = pltpu.make_async_copy(res, res_o, out_sem.at[0])
    out_copy.start()
    vec_o[...] = vec[...]
    for i in range(count):

        @pl.when(core_bit != i % 2)
        def _(i=i):
            for copy in to_sib(i):
                copy.wait_send()

    out_copy.wait()


def finish(res, mixed, gtok, vec, *outs):
    (mixed_o, gtok_o, gain1_o, bias1_o, gain2_o, bias2_o, qkv_o, qkvb_o, wd_o, db_o, we_o, be_o, wc_o, cb_o) = outs
    step = pl.program_id(0)
    width = res.shape[1]
    heads = wd_o.shape[0] // HD
    band = 4 * HD

    @pl.when(step == 0)
    def _():
        wc_o[...] = res[...].astype(F32)
        mixed_o[...] = mixed[...]
        gtok_o[...] = gtok[...]
        for ref, row in ((gain1_o, 0), (bias1_o, 1), (gain2_o, 2), (bias2_o, 3), (db_o, 4), (cb_o, 4), (be_o, 5)):
            ref[...] = vec[row, :]
        for h in range(heads):
            for c in range(3):
                lo = (3 * h + c) * HD
                qkvb_o[c : c + 1, h * HD : (h + 1) * HD] = vec[6:7, lo : lo + HD]

    @pl.when(step == 1)
    def _():
        we_o[...] = res[...].astype(F32)

    @pl.when(step == 2)
    def _():
        for h in range(heads):
            lo = h * band
            for c in range(3):
                qkv_o[c, h * HD : (h + 1) * HD, :] = res[lo + c * HD : lo + (c + 1) * HD, :].astype(F32)
            wd_o[h * HD : (h + 1) * HD, :] = res[lo + 3 * HD : lo + band, :].astype(F32)


def shards(
    n,
    tokens,
    input_gain,
    input_bias,
    post_gain,
    post_bias,
    query_key_value,
    query_key_value_bias,
    dense_weight,
    dense_bias,
    expand_weight,
    expand_bias,
    contract_weight,
    contract_bias,
    lengths,
    cotangent,
):
    blk, width = tokens.shape
    local = query_key_value.shape[2]
    hidden = expand_weight.shape[1]
    heads = local // HD
    total = 4 * blk
    rounds = n.bit_length() - 2
    swaps = rounds + 3
    cosine, sine = angle_rows(total)
    vmem = pl.BlockSpec(memory_space=pltpu.VMEM)
    smem = pl.BlockSpec(memory_space=pltpu.SMEM)
    hbm = pl.BlockSpec(memory_space=pl.ANY)
    dma = pltpu.SemaphoreType.DMA
    mixed, grad_tokens, res, vec = pl.pallas_call(
        functools.partial(core, n),
        name="core",
        out_shape=(
            jax.ShapeDtypeStruct((blk, width), BF16),
            jax.ShapeDtypeStruct((blk, width), F32),
            jax.ShapeDtypeStruct((3 * width, width), BF16),
            jax.ShapeDtypeStruct((8, width), F32),
        ),
        in_specs=[hbm, hbm, smem] + [vmem] * 7 + [hbm, vmem, hbm, hbm, hbm, vmem, vmem],
        out_specs=[vmem, vmem, hbm, vmem],
        scratch_shapes=[
            pltpu.VMEM((total, width), BF16),
            pltpu.VMEM((total, width), BF16),
            pltpu.VMEM((total, width), BF16),
            pltpu.VMEM((total, width), BF16),
            pltpu.VMEM((3 * local, width), BF16),
            pltpu.VMEM((local, width), BF16),
            pltpu.VMEM((width, hidden), BF16),
            pltpu.VMEM((hidden, width), BF16),
            pltpu.VMEM((3 * local, 1), F32),
            pltpu.VMEM((3 * width, width), F32),
            pltpu.VMEM((3 * width, width), BF16),
            pltpu.VMEM((6, blk, width), BF16),
            pltpu.VMEM((heads, 2 * HD, total), BF16),
            pltpu.VMEM((heads, HD, total), BF16),
            pltpu.VMEM((heads, total, 2 * HD), BF16),
            pltpu.VMEM((heads, HD + 16, total), BF16),
            pltpu.VMEM((heads, total, HD), BF16),
            pltpu.VMEM((heads, HD, total), BF16),
            pltpu.VMEM((LEN, blk), BF16),
            pltpu.VMEM((8, blk), F32),
            pltpu.VMEM((heads, HD, total), F32),
            pltpu.VMEM((heads, HD, total), F32),
            pltpu.VMEM((heads, HD, total), BF16),
            pltpu.VMEM((heads, HD, blk), F32),
            pltpu.VMEM((8, width), F32),
            pltpu.VMEM((swaps, 8, width), F32),
            pltpu.VMEM((7, SUB, width // 2), BF16),
            pltpu.VMEM((7, SUB, width // 2), BF16),
            pltpu.VMEM((7, SUB, width // 2), BF16),
            dma((5 + 3 * heads,)),
            dma((6,)),
            dma((6,)),
            dma((3, 2)),
            dma((3, 2)),
            dma((2 * rounds + 2, len(pieces(n)))),
            dma((2 * rounds + 2, len(pieces(n)))),
            dma((swaps,)),
            dma((swaps,)),
            dma((1,)),
            pltpu.SemaphoreType.REGULAR((2,)),
        ],
        compiler_params=pltpu.CompilerParams(
            vmem_limit_bytes=63 * 2**20, collective_id=0, has_side_effects=True
        ),
    )(
        tokens,
        cotangent,
        lengths,
        input_gain,
        input_bias,
        post_gain,
        post_bias,
        expand_bias,
        dense_bias,
        contract_bias,
        jnp.transpose(query_key_value, (0, 2, 1)),
        query_key_value_bias,
        dense_weight,
        expand_weight,
        contract_weight,
        cosine,
        sine,
    )

    def whole(*shape):
        return pl.BlockSpec(shape, lambda g: (0,) * len(shape))

    vector = jax.ShapeDtypeStruct((width,), F32)
    outs = pl.pallas_call(
        finish,
        name="finish",
        grid=(3,),
        in_specs=[
            pl.BlockSpec((width, width), lambda g: (g, 0)),
            whole(blk, width),
            whole(blk, width),
            whole(8, width),
        ],
        out_specs=[whole(blk, width), whole(blk, width)]
        + [whole(width)] * 4
        + [
            whole(3, local, width),
            whole(3, local),
            whole(local, width),
            whole(width),
            whole(width, hidden),
            whole(hidden),
            whole(hidden, width),
            whole(width),
        ],
        out_shape=(
            jax.ShapeDtypeStruct((blk, width), BF16),
            jax.ShapeDtypeStruct((blk, width), F32),
            vector,
            vector,
            vector,
            vector,
            jax.ShapeDtypeStruct((3, local, width), F32),
            jax.ShapeDtypeStruct((3, local), F32),
            jax.ShapeDtypeStruct((local, width), F32),
            vector,
            jax.ShapeDtypeStruct((width, hidden), F32),
            jax.ShapeDtypeStruct((hidden,), F32),
            jax.ShapeDtypeStruct((hidden, width), F32),
            vector,
        ),
        compiler_params=pltpu.CompilerParams(vmem_limit_bytes=63 * 2**20),
    )(res, mixed, grad_tokens, vec)
    outs = list(outs)
    outs[6] = jnp.transpose(outs[6], (0, 2, 1))
    return tuple(outs)


def solution(mesh):
    rows = P(("dp", "tensor"), None)
    weights = (
        P(None, None, "tensor"),
        P(None, "tensor"),
        P("tensor", None),
        P(),
        P(None, "tensor"),
        P("tensor"),
        P("tensor", None),
        P(),
    )
    return jax.shard_map(
        functools.partial(shards, mesh.shape["dp"]),
        mesh=mesh,
        in_specs=(rows, P(), P(), P(), P()) + weights + (P("dp"), rows),
        out_specs=(rows, rows, P(), P(), P(), P()) + weights,
        check_vma=False,
    )
```

time: 184 us -> 166 us (0.902)
  local copies, waits for them, and re-layouts: 13.4 us -> 0 us
  other arithmetic: 5.45 us -> 0 us
    pallas_call x0 -> x1, Pallas kernels: none -> 7.5 us  [shards(): pl.pallas_call(finish, name='finish', grid=(3,), in_specs=[pl.BlockSpec((...]
    pallas_call x1, Pallas kernels: 164 us -> 157 us  [shards(): pl.pallas_call(functools.partial(core, n), name='core', out_shape=(jax.Sh...]
    unnamed x12 -> x0, local copies, waits for them, and re-layouts: 4.95 us -> none
    another operation x8 -> x0, local copies, waits for them, and re-layouts: 4.76 us -> none  [the longest x7 4.09 us: shards(): jnp.stack([input_gain, input_bias, post_gain, post_bias, expand_bias, den...]
    convert_element_type x3 -> x0, other arithmetic: 4.75 us -> none  [the longest x1 2.54 us: shards(): res[0].astype(F32)]
    slice x3 -> x0, local copies, waits for them, and re-layouts: 3.73 us -> none  [the longest x1 1.62 us: shards(): vec[5]]
where the time goes in v3:
time: 166 us; the launch traced here: 165 us
  Pallas kernels  164 us (99%)
    pallas_call x1, Pallas kernels, shards(): pl.pallas_call(functools.partial(core, n), name='core', out_shape=(jax.Sh...  157 us
    pallas_call x1, Pallas kernels, shards(): pl.pallas_call(finish, name='finish', grid=(3,), in_specs=[pl.BlockSpec((...  7.5 us

profile of v3, /device:TPU:0, one launch (start us, length us, event | category | flops | bytes accessed | tf_op | source)
XLA Modules:
  0.0 165.4 jit_solution(11549956283966672657)
XLA Ops:
  1.3 156.6 %core.1 = (bf16[512,768]{1,0:T(8,128)(2,1)}, f32[512,768]{1,0:T(8,128)}, bf16[2304,768]{1,0:T(8,128)(2,1)}, f32[8,768]{1,0:T(8,128)}) custom-call(bf16[512,768]{1,0:T(8,128)(2,1)} %tok.1, bf16[512,768]{1,0:T(8,128)(2,1)} %cot.1, s32[1]{0:T(128)S(6)} %copy.31.len_ref, f32[768]{0:T(1024)} %gain1_r.1, f32[768]{0:T(1024)} %bias1_r.1, f32[768]{0:T(1024)} %gain2_r.1, ...), custom_call_target="tpu_custom_call" | custom-call | tf_op jit(solution)/shard_map/core/pallas_call | solution.py:764
  157.9 7.5 %finish.1 = (bf16[512,768]{1,0:T(8,128)(2,1)}, f32[512,768]{1,0:T(8,128)}, f32[768]{0:T(1024)}, f32[768]{0:T(1024)}, f32[768]{0:T(1024)}, /*index=5*/f32[768]{0:...) custom-call(bf16[2304,768]{1,0:T(8,128)(2,1)} %get-tuple-element.32., ...), custom_call_target="tpu_custom_call" | custom-call | tf_op jit(solution)/shard_map/finish/pallas_call | solution.py:844

commit v4 on v3

--- a/solution.py
+++ b/solution.py
@@ -39,7 +39,9 @@
 
 MESH = pl.DeviceIdType.MESH
 SUB = 256
-UNIT = 1.25
+UNIT = 1.0
+FRONT = 0.52
+ORDER = (0,)
 
 
 def flip(value, bits):
@@ -51,20 +53,23 @@
     return value
 
 
-def pieces(n):
-    made = [(SUB * k, SUB, k, 0) for k in range(7)]
-    parts = 2 if n <= 16 else 1
-    size = SUB // parts
-    for k in range(2 * parts):
-        made.append((7 * SUB + size * k, size, k // parts, size * (k % parts)))
-    return made
-
-
-def plan(rounds, chunks, points, width, margin=0.4, rate=0.05, delay=2.6, work=0.35):
-    free = [points[0], points[0]]
+def pieces(n, heads):
+    bits = tuple(range(n.bit_length() - 1))
+    orders = (bits, bits[1:] + bits[:1], bits[1:2] + bits[:1] + bits[2:])
+    count = 6 + heads
+    made = []
+    for k in range(count):
+        parts = 2 if k == count - 1 and n <= 16 else 1
+        size = SUB // parts
+        made += [[SUB * k + size * p, size] for p in range(parts)]
+    return [(a, b, orders[ORDER[k % len(ORDER)]]) for k, (a, b) in enumerate(made)]
+
+
+def plan(chunks, ready, points, width, margin=0.5, rate=0.045, delay=3.0, work=0.2):
+    free = {}
     clock = points[0]
     reached = 0
-    todo = [(when, k, 0) for k, (when, _) in enumerate(chunks)]
+    todo = [(when, k, 0) for k, when in enumerate(ready)]
     made = []
     while todo:
         todo.sort()
@@ -72,19 +77,22 @@
         later = [(at, u) for u, at in enumerate(points) if at >= when and u >= reached]
         if later:
             at, reached = later[0]
-            u = reached
             clock = max(at, clock)
         else:
-            u = reached = len(points)
+            reached = len(points)
             clock = max(when, clock, points[-1] + 1.5)
         clock += work
-        made.append((clock, u, k, step))
-        if step < 2 * rounds + 2:
-            size = chunks[k][1] * width * 1e-6
-            turn = min(step, 2 * rounds + 1 - step)
-            kind = 1 if turn else 0
-            free[kind] = max(free[kind], clock) + size / 2**turn / rate
-            todo.append((free[kind] + delay + (margin if later else 0.0), k, step + 1))
+        made.append((clock, reached, k, step))
+        _, rows, order = chunks[k]
+        if step < 2 * len(order):
+            turn = min(step, 2 * len(order) - 1 - step)
+            cost = rows * width * 2e-6 / 2 ** (turn + 1) / rate
+            uses = {0: {"x": 1}, 1: {"end": 1}}.get(order[turn], {"end": 1, "mid": 2})
+            through = clock
+            for link, share in uses.items():
+                free[link] = max(free.get(link, points[0]), clock) + share * cost
+                through = max(through, free[link])
+            todo.append((through + delay + (margin if later else 0.0), k, step + 1))
     return made
 
 
@@ -129,17 +137,14 @@
     va,
     vr,
     dot_s,
-    pt,
-    mrun,
+    lse,
     dkt,
     dvt,
     ctx_s,
-    dq_s,
     vec,
     vec_in,
     sx,
     rx,
-    rz,
     in_sem,
     ag_send,
     ag_recv,
@@ -161,14 +166,14 @@
     root = HD**-0.5
     band = 4 * HD
     attn = 2 * width
-    rounds = n.bit_length() - 2
+    bits = n.bit_length() - 1
     dp = lax.axis_index("dp")
     t = lax.axis_index("tensor")
     core_bit = t % 2
     chip_bit = t // 2
     sib = (dp, flip(t, 1))
     across = (dp, flip(t, 2))
-    peers = [(flip(dp, 2**q), t) for q in range(rounds + 1)]
+    peers = [(flip(dp, 2**q), t) for q in range(bits)]
 
     def send(src, dst, ssem, rsem, where):
         return pltpu.make_async_remote_copy(
@@ -229,7 +234,7 @@
         column = jnp.transpose(jnp.broadcast_to(qkv_b[c : c + 1, :], (8, local)))
         for h in range(heads):
             qb_s[(3 * h + c) * HD : (3 * h + c + 1) * HD, :] = column[h * HD : (h + 1) * HD, :1]
-    for ref in (acc, vec, dkt, dvt):
+    for ref in (acc, vec):
         ref[...] = jnp.zeros_like(ref)
     one_row = (lax.broadcasted_iota(jnp.int32, (heads, HD, total), 1) == 0).astype(F32)
     qa[:, HD:, :] = one_row.astype(BF16)
@@ -237,102 +242,78 @@
     for copy in fetch:
         copy.wait()
 
-    half = width // 2
-    near_bit = dp % 2
-    seat = dp // 2
-
-    def lanes(bit):
-        return pl.ds(pl.multiple_of(bit * half, 128), half)
-
-    my_lanes = lanes(near_bit)
-    chunks = pieces(n)
+    chunks = pieces(n, heads)
+
+    def rows_of(k, first, size):
+        step = min(chunks[k][1] // n, 128)
+        return pl.ds(pl.multiple_of(chunks[k][0] + first, step), size)
 
     def first_of(k, q):
         first = 0
         for p in range(q):
-            first = first + ((seat // 2**p) % 2) * (chunks[k][1] // 2 ** (p + 1))
+            first = first + ((dp // 2 ** chunks[k][2][p]) % 2) * (chunks[k][1] // 2 ** (p + 1))
         return first
 
-    def span(k, q, first):
+    def kept(k, q):
+        return rows_of(k, first_of(k, q), chunks[k][1] // 2**q)
+
+    def given(k, q):
         size = chunks[k][1] // 2**q
-        return pl.ds(pl.multiple_of(chunks[k][0] + first, chunks[k][1] // 2**rounds), size)
-
-    def kept(k, q):
-        return span(k, q, first_of(k, q))
-
-    def given(k, q):
-        bit = (seat // 2 ** (q - 1)) % 2
-        return span(k, q, first_of(k, q - 1) + (1 - bit) * (chunks[k][1] // 2**q))
-
-    def whole_slot(k):
-        _, rows, slot, low = chunks[k]
-        return slot, pl.ds(low, rows)
-
-    def slot_part(k, q):
-        _, rows, slot, low = chunks[k]
-        return slot, pl.ds(low + rows - rows // 2 ** (q - 1), rows // 2**q)
+        bit = (dp // 2 ** chunks[k][2][q - 1]) % 2
+        return rows_of(k, first_of(k, q - 1) + (1 - bit) * size, size)
+
+    def landing(k, q):
+        first, rows, _ = chunks[k]
+        return pl.ds(first + rows - rows // 2 ** (q - 1), rows // 2**q)
 
     def ar_copy(k, step):
         sems = (ar_send.at[step, k], ar_recv.at[step, k])
-        if step == 0:
-            return send(sx.at[whole_slot(k)], rx.at[whole_slot(k)], *sems, peers[0])
-        if step <= rounds:
-            return send(sx.at[slot_part(k, step)], rz.at[slot_part(k, step)], *sems, peers[step])
-        if step <= 2 * rounds:
-            q = 2 * rounds - step + 1
-            piece = res.at[kept(k, q), my_lanes]
-            return send(piece, piece, *sems, peers[q])
-        piece = res.at[kept(k, 0), my_lanes]
-        return send(piece, piece, *sems, peers[0])
+        order = chunks[k][2]
+        if step < bits:
+            return send(sx.at[landing(k, step + 1)], rx.at[landing(k, step + 1)], *sems, peers[order[step]])
+        q = 2 * bits - step
+        piece = res.at[kept(k, q)]
+        return send(piece, piece, *sems, peers[order[q - 1]])
 
     def advance(k, step):
-        if step == 0:
-            sx[whole_slot(k)] = acc[kept(k, 0), lanes(1 - near_bit)].astype(BF16)
-        else:
+        if step > 0:
             ar_copy(k, step - 1).wait()
-        if step == 1:
-            mine = kept(k, 0)
-            acc[mine, my_lanes] = acc[mine, my_lanes] + rx[whole_slot(k)].astype(F32)
-        if 2 <= step <= rounds + 1:
-            mine = kept(k, step - 1)
-            done = acc[mine, my_lanes] + rz[slot_part(k, step - 1)].astype(F32)
-            if step <= rounds:
-                acc[mine, my_lanes] = done
+        if 1 <= step <= bits:
+            mine = kept(k, step)
+            done = acc[mine, :] + rx[landing(k, step), :].astype(F32)
+            if step < bits:
+                acc[mine, :] = done
             else:
-                res[mine, my_lanes] = done.astype(BF16)
-        if 1 <= step <= rounds:
-            sx[slot_part(k, step)] = acc[given(k, step), my_lanes].astype(BF16)
-        if step < 2 * rounds + 2:
+                res[mine, :] = done.astype(BF16)
+        if step < bits:
+            sx[landing(k, step + 1), :] = acc[given(k, step + 1), :].astype(BF16)
+        if step < 2 * bits:
             ar_copy(k, step).start()
 
-    clock = -7.0
-    points = [-7.0, -5.0, -3.2, -1.6]
+    first_it = 9
+    points = [-14.2, -12.3, -10.4, -8.9]
+    lead = len(points)
+    points += [-7.4 + FRONT * (u + 1) for u in range(heads * count)]
+    mid = len(points)
+    ends = []
     clock = 0.0
-    for group in (1, heads - 1):
+    for h in range(heads):
         for i in range(count - 1, -1, -1):
-            for _ in range(group * (i + 1)):
+            for _ in range(i + 1):
                 clock += UNIT
                 points.append(clock)
-            clock += 0.9 if group == 1 else 2.2
-            if group == 1 and i == 0:
-                first_head = clock
+            clock += 0.7 if h < heads - 1 else 1.6
+        ends.append(clock)
     last_time = clock
-    ready = [points[0]] * 3 + [points[2]] * 3 + [first_head]
-    begin = last_time
-    while True:
-        times = ready + [begin] * (len(chunks) - len(ready))
-        made = plan(rounds, [(r, c[1]) for r, c in zip(times, chunks)], points, width)
-        through = max(at for at, (_, _, k, step) in enumerate(made) if k < 2)
-        if through < min(at for at, (_, _, k, _) in enumerate(made) if k > 6):
-            break
-        begin = max(begin, made[through][0]) + 0.1
+    ready = [points[0]] * 3 + [points[2]] * 3 + ends
+    ready += [last_time] * (len(chunks) - len(ready))
     ticks = {}
     after = []
-    for when, u, k, step in made:
+    for when, u, k, step in plan(chunks, ready, points, width):
         if u < len(points):
-            ticks.setdefault(u, []).append((k, step))
+            ticks.setdefault(u, []).append(functools.partial(advance, k, step))
         else:
-            after.append((when, k, step))
+            after.append((when, functools.partial(advance, k, step)))
 
     def forward(b, slot, before_mix):
         rows = block(b)
@@ -380,10 +361,56 @@
         high = (t // 2 + k // 2) % 2
         return low + 2 * high
 
+    key_i = lax.broadcasted_iota(jnp.int32, (blk, blk), 0)
+    query_i = lax.broadcasted_iota(jnp.int32, (blk, blk), 1)
+
+    def serve(unit, low, high):
+        for u, jobs in ticks.items():
+            if low <= u < high:
+
+                @pl.when(unit == u)
+                def _(jobs=jobs):
+                    for job in jobs:
+                        job()
+
+    def front(i):
+        passed = jnp.where(i == count - 1, lead, -mid)
+        base = (i // per) * per
+        mine = block(i)
+
+        def head(h, _):
+            q_aug = qa[h, :, mine]
+
+            def weigh(j, scores, high, out):
+                top = jnp.max(jnp.max(scores.reshape(blk // 8, 8, blk), 0), 0, keepdims=True)
+                top = jnp.maximum(high, top)
+                p = jnp.exp(scores - top).astype(BF16)
+                return top, out * jnp.exp(high - top) + dot(va[h, :, block(j)], p, 1, 0)
+
+            def onward(j, carry):
+                more = weigh(j, dot(kr[h, block(j), :], q_aug, 1, 0), *carry)
+                serve(passed + h * count + (j - base), lead, mid)
+                return more
+
+            begin = (jnp.full((1, blk), MASKED, F32), jnp.zeros((va.shape[1], blk), F32))
+            carry = lax.fori_loop(base, i, onward, begin)
+            scores = dot(kr[h, mine, :], q_aug, 1, 0)
+            high, out = weigh(i, jnp.where(key_i <= query_i, scores, MASKED), *carry)
+            norm = out[HD : HD + 1]
+            ctx_s[h, :, mine] = (out[:HD] * (1.0 / norm)).astype(BF16)
+            lse[pl.ds(h, 1), mine] = high + jnp.log(norm)
+            serve(passed + h * count + (i - base), lead, mid)
+            return 0
+
+        lax.fori_loop(0, heads, head, 0)
+        ctx = ctx_s[:, :, mine].reshape(local, blk)
+        mix = dot(ctx, wd[...], 0, 0) + x_s[mine, :].astype(F32)
+        x_s[mine, :] = mix.astype(BF16)
+
     def phase(it, _):
-        late = it // 4 > 0
-        b = mate(jnp.where(late, 2 + it % 2, it))
-        slot = jnp.where(late, it % 2, it // 3)
+        late = it // 7 > 0
+        b = mate(jnp.where(late, 2 + (it + 1) % 2, it % 4))
+        slot = jnp.where(late, (it + 1) % 2, (it % 4) // 3)
         rows = block(b)
 
         @pl.when(it == 1)
@@ -411,27 +438,26 @@
 
             forward(b, slot, settle)
 
-        @pl.when(it == 4)
+        @pl.when(((it > 3) & (it < 7)) | (it == 13))
+        def _():
+            front(jnp.where(late, count - 1, it - 4))
+
+        @pl.when(it == 7)
         def _():
             gather[1].wait_recv()
             gather[5].start()
 
-        @pl.when(it == 5)
+        @pl.when(it == 8)
         def _():
             gather[5].wait_recv()
 
-        for u in range(4):
-
-            @pl.when(it == 6 + u)
-            def _(u=u):
-                for k, at in ticks.get(u, ()):
-                    advance(k, at)
-
-        @pl.when((it < 2) | (it == 4) | (it == 5))
+        serve(it - first_it, 0, lead)
+
+        @pl.when((it < 2) | (it == 7) | (it == 8))
         def _():
             acc[:width] += dot(hold[slot], g_s[rows, :], 0, 0)
 
-        @pl.when((it < 2) | (it == 6) | (it == 7))
+        @pl.when((it < 2) | (it == 9) | (it == 10))
         def _():
             slope = hold[4 + slot].astype(F32)
             grad_pre = (dot(g_s[rows, :], wc[...], 1, 1) * slope).astype(BF16)
@@ -439,7 +465,7 @@
             vec[5:6, :] += jnp.sum(grad_pre.astype(F32), 0, keepdims=True)
             acc[width : 2 * width] += dot(hold[2 + slot], grad_pre, 0, 0)
 
-        @pl.when((it < 2) | (it > 7))
+        @pl.when((it < 2) | (it == 11) | (it == 12))
         def _():
             part = dot(hold[slot], we[...], 1, 1)
             s_s[rows, :] = (part * gain2).astype(BF16)
@@ -451,122 +477,106 @@
 
         return 0
 
-    lax.fori_loop(0, 10, phase, 0)
+    lax.fori_loop(0, 14, phase, 0)
     for k in (1, 2, 3, 5):
         gather[k].wait_send()
     pl.semaphore_signal(free_sem.at[0], inc=1, device_id=sib, device_id_type=MESH)
     pl.semaphore_signal(free_sem.at[1], inc=1, device_id=across, device_id_type=MESH)
 
-    def to_sib(i):
-        rows = block(i)
+    def dense_grad(i, _):
+        grad_d = dot(ctx_s[:, :, block(i)].reshape(local, blk), g_s[block(i), :], 1, 0)
+        for h in range(heads):
+            at = attn + h * band + 3 * HD
+            acc[at : at + HD, :] += grad_d[h * HD : (h + 1) * HD]
+        return 0
+
+    lax.fori_loop(0, count, dense_grad, 0)
+
+    sums = (x_s, s_s)
+
+    def to_sib(i, w):
         slot = i // 2
-        return [
-            send(x_s.at[rows], hold.at[2 * slot], rs_send.at[slot, 0], rs_recv.at[slot, 0], sib),
-            send(s_s.at[rows], hold.at[2 * slot + 1], rs_send.at[slot, 1], rs_recv.at[slot, 1], sib),
-        ]
-
-    def to_owner(i):
-        rows = block(i)
-        return [
-            send(x_s.at[rows], hold.at[4], rs_send.at[2, 0], rs_recv.at[2, 0], across),
-            send(s_s.at[rows], hold.at[5], rs_send.at[2, 1], rs_recv.at[2, 1], across),
-        ]
-
-    def hand_over(i):
+        src = sums[w].at[block(i)]
+        return send(src, hold.at[2 * slot + w], rs_send.at[slot, w], rs_recv.at[slot, w], sib)
+
+    def to_owner(i, w):
+        src = sums[w].at[block(i)]
+        return send(src, hold.at[4 + w], rs_send.at[2, w], rs_recv.at[2, w], across)
+
+    def hand_over(i, w):
         @pl.when(core_bit != i % 2)
         def _():
-            for copy in to_sib(i):
-                copy.start()
-
-    def pass_on(i):
+            to_sib(i, w).start()
+
+    def pass_on(i, w):
         @pl.when(core_bit == i % 2)
         def _():
-            for copy in to_sib(i):
-                copy.wait_recv()
+            to_sib(i, w).wait_recv()
 
         @pl.when((core_bit == i % 2) & (chip_bit != i // 2))
         def _():
             rows = block(i)
-            slot = i // 2
-            for w, ref in enumerate((x_s, s_s)):
-                both = ref[rows, :].astype(F32) + hold[2 * slot + w].astype(F32)
-                ref[rows, :] = both.astype(BF16)
-            for copy in to_owner(i):
-                copy.start()
-
-    key_i = lax.broadcasted_iota(jnp.int32, (blk, blk), 0)
-    query_i = lax.broadcasted_iota(jnp.int32, (blk, blk), 1)
-
-    def gain_sum(some):
-        for h in some:
-            w32 = wt[3 * h * HD : 3 * (h + 1) * HD, :].astype(F32)
-            mine = acc[attn + h * band : attn + h * band + 3 * HD, :]
-            vec[0:1, :] += jnp.sum(w32 * mine, 0, keepdims=True)
+            both = sums[w][rows, :].astype(F32) + hold[2 * (i // 2) + w].astype(F32)
+            sums[w][rows, :] = both.astype(BF16)
+            to_owner(i, w).start()
+
+    def mixes_over():
+        pl.semaphore_wait(free_sem.at[0], 1)
+        pl.semaphore_wait(free_sem.at[1], 1)
+
+        def one(i, _):
+            hand_over(i, 0)
+            return 0
+
+        lax.fori_loop(0, count, one, 0)
+
+    def mixes_on():
+        def one(i, _):
+            pass_on(i, 0)
+            return 0
+
+        lax.fori_loop(0, count, one, 0)
+
+    ticks.setdefault(mid + 3, []).insert(0, mixes_over)
+    ticks.setdefault(mid + 7, []).insert(0, mixes_on)
 
     def attend(visit, _):
-        group = visit // count
-        step = visit % count
-        i = count - 1 - step
+        h = visit // count
+        i = count - 1 - visit % count
         base = (i // per) * per
         mine = block(i)
-        size = 1 + group * (heads - 2)
-        passed = size * (count * step - (step * (step - 1)) // 2)
-        passed += 4 + group * (count * (count + 1) // 2)
-
-        def head(h, _):
-            q_aug = qa[h, :, mine]
-
-            def weigh(j, s, high, out):
-                top = jnp.max(jnp.max(s.reshape(blk // 8, 8, blk), 0), 0, keepdims=True)
-                top = jnp.maximum(high, top)
-                p = jnp.exp(s - top).astype(BF16)
-                pt[block(j - base), :] = p
-                mrun[pl.ds(j - base, 1), :] = top
-                return top, out * jnp.exp(high - top) + dot(va[h, :, block(j)], p, 1, 0)
-
-            def onward(j, carry):
-                return weigh(j, dot(kr[h, block(j), :], q_aug, 1, 0), *carry)
-
-            begin = (jnp.full((1, blk), MASKED, F32), jnp.zeros((va.shape[1], blk), F32))
-            carry = lax.fori_loop(base, i, onward, begin)
-            s = dot(kr[h, mine, :], q_aug, 1, 0)
-            high, out = weigh(i, jnp.where(key_i <= query_i, s, MASKED), *carry)
-            scale = 1.0 / out[HD : HD + 1]
-            ctx = out[:HD] * scale
-            ctx_s[h, :, mine] = ctx.astype(BF16)
-            grad = dot_s[h, :, mine].astype(F32) * scale
-            q = q_aug[:HD]
-
-            def back(j, dq):
-                cols = block(j)
-                p = pt[block(j - base), :]
-                go = (grad * jnp.exp(mrun[pl.ds(j - base, 1), :] - high)).astype(BF16)
-                inner = jnp.sum(ctx * go.astype(F32), 0, keepdims=True)
-                dvt[h, :, cols] += dot(go, p, 1, 1)
-                dp_t = dot(vr[h, cols, :], go, 1, 0)
-                ds = (p.astype(F32) * (dp_t - inner)).astype(BF16)
-                dkt[h, :, cols] += dot(q, ds, 1, 1)
-                unit = passed + (h - group) * (i + 1) + (j - base)
-                for u, steps in ticks.items():
-                    if u < 4:
-                        continue
-
-                    @pl.when(unit == u)
-                    def _(steps=steps):
-                        for k, at in steps:
-                            advance(k, at)
-
-                return dq + dot(kt[h, :, cols], ds, 1, 0)
-
-            dq_s[h] = lax.fori_loop(base, i + 1, back, jnp.zeros((HD, blk), F32))
-
-            @pl.when((h == 1) & (step > 0))
-            def _():
-                pass_on(i + 1)
-
-            return 0
-
-        lax.fori_loop(group, group + size, head, 0)
+        passed = h * (count * (count + 1) // 2) + mid
+        passed += count * (count - 1 - i) - ((count - 1 - i) * (count - 2 - i)) // 2
+
+        @pl.when(i == count - 1)
+        def _():
+            dkt[...] = jnp.zeros_like(dkt)
+            dvt[...] = jnp.zeros_like(dvt)
+
+        q_aug = qa[h, :, mine]
+        q = q_aug[:HD]
+        go = dot_s[h, :, mine]
+        total_log = lse[pl.ds(h, 1), mine]
+        inner = jnp.sum(ctx_s[h, :, mine].astype(F32) * go.astype(F32), 0, keepdims=True)
+
+        def back(j, scores):
+            cols = block(j)
+            p = jnp.exp(scores - total_log)
+            dvt[:, cols] += dot(go, p.astype(BF16), 1, 1)
+            dp_t = dot(vr[h, cols, :], go, 1, 0)
+            ds = (p * (dp_t - inner)).astype(BF16)
+            dkt[:, cols] += dot(q, ds, 1, 1)
+            return dot(kt[h, :, cols], ds, 1, 0)
+
+        def onward(j, dq):
+            more = back(j, dot(kr[h, block(j), :], q_aug, 1, 0))
+            serve(passed + (j - base), mid, len(points))
+            return dq + more
+
+        dq = lax.fori_loop(base, i, onward, jnp.zeros((HD, blk), F32))
+        scores = dot(kr[h, mine, :], q_aug, 1, 0)
+        dq += back(i, jnp.where(key_i <= query_i, scores, MASKED))
+        serve(passed + (i - base), mid, len(points))
         cosine = cos_t[:, mine]
         sine = sin_t[:, mine]
 
@@ -577,55 +587,36 @@
                 [a * cosine + c * sine, c * cosine - a * sine, rows_in[ROT:]], 0
             )
 
-        def projected(some):
-            parts = [(qa[h, :HD, mine], kt[h, :, mine], va[h, :HD, mine]) for h in some]
-            return jnp.concatenate([x for three in parts for x in three], 0)
-
-        def weights(some):
-            for h in some:
-                qa[h, :HD, mine] = unturn(dq_s[h] * root).astype(BF16)
-                kt[h, :, mine] = unturn(dkt[h, :, mine]).astype(BF16)
-                va[h, :HD, mine] = dvt[h, :, mine].astype(BF16)
-            lo, hi = some[0], some[-1] + 1
-            ctx = ctx_s[lo:hi, :, mine].reshape((hi - lo) * HD, blk)
-            grad_proj = projected(some)
-            grad_d = dot(ctx, g_s[mine, :], 1, 0)
-            grad_w = dot(grad_proj, n1_s[mine, :], 1, 0)
-            for h in some:
-                at = attn + h * band
-                acc[at : at + 3 * HD, :] += grad_w[3 * (h - lo) * HD : 3 * (h - lo + 1) * HD]
-                acc[at + 3 * HD : at + band, :] += grad_d[(h - lo) * HD : (h - lo + 1) * HD]
-
-        @pl.when(group == 0)
-        def _():
-            weights([0])
-
-            @pl.when(step == count - 1)
+        qa[h, :HD, mine] = unturn(dq * root).astype(BF16)
+        kt[h, :, mine] = unturn(dkt[:, mine]).astype(BF16)
+        va[h, :HD, mine] = dvt[:, mine].astype(BF16)
+        grad_proj = jnp.concatenate([qa[h, :HD, mine], kt[h, :, mine], va[h, :HD, mine]], 0)
+        at = attn + h * band
+        acc[pl.ds(pl.multiple_of(at, HD), 3 * HD), :] += dot(grad_proj, n1_s[mine, :], 1, 0)
+
+        @pl.when(i == 0)
+        def _():
+            w32 = wt[pl.ds(pl.multiple_of(3 * h * HD, HD), 3 * HD), :].astype(F32)
+            grads = acc[pl.ds(pl.multiple_of(at, HD), 3 * HD), :]
+            vec[0:1, :] += jnp.sum(w32 * grads, 0, keepdims=True)
+
+        @pl.when(h == heads - 1)
+        def _():
+            @pl.when(i < count - 1)
             def _():
-                gain_sum([0])
-
-        @pl.when(group == 1)
-        def _():
-            weights(list(range(1, heads)))
-            ctx = ctx_s[:, :, mine].reshape(local, blk)
-            mix = dot(ctx, wd[...], 0, 0) + x_s[mine, :].astype(F32)
-            x_s[mine, :] = mix.astype(BF16)
-            grad_proj = projected(range(heads))
-            part = dot(grad_proj, wt[...], 0, 0) * gain1 + s_s[mine, :].astype(F32)
+                pass_on(i + 1, 1)
+
+            parts = [(qa[g, :HD, mine], kt[g, :, mine], va[g, :HD, mine]) for g in range(heads)]
+            every = jnp.concatenate([x for three in parts for x in three], 0)
+            part = dot(every, wt[...], 0, 0) * gain1 + s_s[mine, :].astype(F32)
             s_s[mine, :] = part.astype(BF16)
-
-            @pl.when(step == 0)
-            def _():
-                pl.semaphore_wait(free_sem.at[0], 1)
-                pl.semaphore_wait(free_sem.at[1], 1)
-
-            hand_over(i)
+            hand_over(i, 1)
             ones = jnp.ones((8, blk), BF16)
-            vec[6:7, : 3 * local] += dot(ones, grad_proj, 1, 1)[:1]
+            vec[6:7, : 3 * local] += dot(ones, every, 1, 1)[:1]
 
         return 0
 
-    lax.fori_loop(0, 2 * count, attend, 0)
+    lax.fori_loop(0, heads * count, attend, 0)
     again = pltpu.make_async_copy(tok, n1_s.at[own], in_sem.at[0])
     again.start()
 
@@ -648,15 +639,14 @@
         w32 = wt[...].astype(F32)
         column = jnp.transpose(jnp.broadcast_to(vec[6:7, : 3 * local], (8, 3 * local)))[:, :1]
         grad_bias = jnp.sum(w32 * column, 0, keepdims=True)
-        gain_sum(range(1, heads))
         vec[1:2, :] = grad_bias
         vec[0:1, :] = (vec[0:1, :] - bias1 * grad_bias) / gain1
         vec[2:3, :] = (vec[2:3, :] - bias2 * vec[3:4, :]) / gain2
         vec[4:5, :] = jnp.sum(g_s[own, :].astype(F32), 0, keepdims=True)
 
     def tokens_out():
-        for copy in to_owner(flip(t, 2)):
-            copy.wait()
+        for w in range(2):
+            to_owner(flip(t, 2), w).wait()
         again.wait()
         rows = n1_s[own, :]
         mix = rows.astype(F32) + (outb1_r[...] + outb2_r[...]).reshape(1, width)
@@ -671,9 +661,9 @@
             s - jnp.mean(s, -1, keepdims=True) - unit * jnp.mean(s * unit, -1, keepdims=True)
         )
 
-    jobs = [(when, functools.partial(advance, k, step)) for when, k, step in after]
+    jobs = list(after)
     jobs.append((last_time + 2.9, vectors))
-    jobs.append((last_time + 3.0, functools.partial(pass_on, 0)))
+    jobs.append((last_time + 3.0, functools.partial(pass_on, 0, 1)))
     for q in range(len(swaps)):
 
         def trade(q=q):
@@ -683,7 +673,7 @@
 
         jobs.append((last_time + 4.0 + 3.5 * q, trade))
     jobs.append((last_time + 4.0 + 3.5 * len(swaps), lambda: finish_swap(len(swaps) - 1)))
-    jobs.append((last_time + 32.0, tokens_out))
+    jobs.append((last_time + 20.0, tokens_out))
     for _, job in sorted(jobs, key=lambda pair: pair[0]):
         job()
     out_copy = pltpu.make_async_copy(res, res_o, out_sem.at[0])
@@ -693,8 +683,8 @@
 
         @pl.when(core_bit != i % 2)
         def _(i=i):
-            for copy in to_sib(i):
-                copy.wait_send()
+            for w in range(2):
+                to_sib(i, w).wait_send()
 
     out_copy.wait()
 
@@ -754,8 +744,9 @@
     hidden = expand_weight.shape[1]
     heads = local // HD
     total = 4 * blk
-    rounds = n.bit_length() - 2
-    swaps = rounds + 3
+    bits = n.bit_length() - 1
+    swaps = bits + 2
+    parts = len(pieces(n, heads))
     cosine, sine = angle_rows(total)
     vmem = pl.BlockSpec(memory_space=pltpu.VMEM)
     smem = pl.BlockSpec(memory_space=pltpu.SMEM)
@@ -791,24 +782,21 @@
             pltpu.VMEM((heads, HD + 16, total), BF16),
             pltpu.VMEM((heads, total, HD), BF16),
             pltpu.VMEM((heads, HD, total), BF16),
-            pltpu.VMEM((LEN, blk), BF16),
-            pltpu.VMEM((8, blk), F32),
-            pltpu.VMEM((heads, HD, total), F32),
-            pltpu.VMEM((heads, HD, total), F32),
+            pltpu.VMEM((8, total), F32),
+            pltpu.VMEM((HD, total), F32),
+            pltpu.VMEM((HD, total), F32),
             pltpu.VMEM((heads, HD, total), BF16),
-            pltpu.VMEM((heads, HD, blk), F32),
             pltpu.VMEM((8, width), F32),
             pltpu.VMEM((swaps, 8, width), F32),
-            pltpu.VMEM((7, SUB, width // 2), BF16),
-            pltpu.VMEM((7, SUB, width // 2), BF16),
-            pltpu.VMEM((7, SUB, width // 2), BF16),
+            pltpu.VMEM((3 * width, width), BF16),
+            pltpu.VMEM((3 * width, width), BF16),
             dma((5 + 3 * heads,)),
             dma((6,)),
             dma((6,)),
             dma((3, 2)),
             dma((3, 2)),
-            dma((2 * rounds + 2, len(pieces(n)))),
-            dma((2 * rounds + 2, len(pieces(n)))),
+            dma((2 * bits, parts)),
+            dma((2 * bits, parts)),
             dma((swaps,)),
             dma((swaps,)),
             dma((1,)),

time: 166 us -> 150 us (0.904)
  Pallas kernels: 164 us -> 149 us
    pallas_call x1, Pallas kernels: 157 us -> 141 us  [shards(): pl.pallas_call(functools.partial(core, n), name='core', out_shape=(jax.Sh...]
where the time goes in v4:
time: 150 us
  Pallas kernels  149 us (99%)
    pallas_call x1, Pallas kernels, shards(): pl.pallas_call(functools.partial(core, n), name='core', out_shape=(jax.Sh...  141 us
    pallas_call x1, Pallas kernels, shards(): pl.pallas_call(finish, name='finish', grid=(3,), in_specs=[pl.BlockSpec((...  7.5 us

profile of v4, /device:TPU:0, one launch (start us, length us, event | category | flops | bytes accessed | tf_op | source)
XLA Modules:
  0.0 150.1 jit_solution(12440267676663981202)
XLA Ops:
  1.3 141.3 %core.1 = (bf16[512,768]{1,0:T(8,128)(2,1)}, f32[512,768]{1,0:T(8,128)}, bf16[2304,768]{1,0:T(8,128)(2,1)}, f32[8,768]{1,0:T(8,128)}) custom-call(bf16[512,768]{1,0:T(8,128)(2,1)} %tok.1, bf16[512,768]{1,0:T(8,128)(2,1)} %cot.1, s32[1]{0:T(128)S(6)} %copy.31.len_ref, f32[768]{0:T(1024)} %gain1_r.1, f32[768]{0:T(1024)} %bias1_r.1, f32[768]{0:T(1024)} %gain2_r.1, ...), custom_call_target="tpu_custom_call" | custom-call | tf_op jit(solution)/shard_map/core/pallas_call | solution.py:755
  142.6 7.5 %finish.1 = (bf16[512,768]{1,0:T(8,128)(2,1)}, f32[512,768]{1,0:T(8,128)}, f32[768]{0:T(1024)}, f32[768]{0:T(1024)}, f32[768]{0:T(1024)}, /*index=5*/f32[768]{0:...) custom-call(bf16[2304,768]{1,0:T(8,128)(2,1)} %get-tuple-element.32., ...), custom_call_target="tpu_custom_call" | custom-call | tf_op jit(solution)/shard_map/finish/pallas_call | solution.py:832

commit v5 on v4

--- a/solution.py
+++ b/solution.py
@@ -41,7 +41,6 @@
 SUB = 256
 UNIT = 1.0
 FRONT = 0.52
-ORDER = (0,)
 
 
 def flip(value, bits):
@@ -54,18 +53,35 @@
 
 
 def pieces(n, heads):
-    bits = tuple(range(n.bit_length() - 1))
-    orders = (bits, bits[1:] + bits[:1], bits[1:2] + bits[:1] + bits[2:])
+    bits = n.bit_length() - 1
     count = 6 + heads
     made = []
+    base = 0
     for k in range(count):
-        parts = 2 if k == count - 1 and n <= 16 else 1
+        last = k == count - 1
+        parts = 2 if last and n <= 16 else 1
         size = SUB // parts
-        made += [[SUB * k + size * p, size] for p in range(parts)]
-    return [(a, b, orders[ORDER[k % len(ORDER)]]) for k, (a, b) in enumerate(made)]
-
-
-def plan(chunks, ready, points, width, margin=0.5, rate=0.045, delay=3.0, work=0.2):
+        depth = max(bits - 2, 1) if last else bits - 1
+        room = size - size // 2**depth + (bits - depth) * (size // 2**depth)
+        for p in range(parts):
+            made.append((SUB * k + size * p, size, depth, base, room))
+            base += room
+    return made
+
+
+def trade_size(rows, depth, bits, step):
+    if step < depth:
+        return rows // 2 ** (step + 1)
+    if step < bits:
+        return rows // 2**depth
+    return rows // 2 ** (depth - (step - bits))
+
+
+def trade_bit(depth, bits, step):
+    return step if step < bits else depth - (step - bits) - 1
+
+
+def plan(bits, chunks, ready, points, width, margin=0.5, rate=0.045, delay=3.0, work=0.2):
     free = {}
     clock = points[0]
     reached = 0
@@ -83,11 +99,10 @@
             clock = max(when, clock, points[-1] + 1.5)
         clock += work
         made.append((clock, reached, k, step))
-        _, rows, order = chunks[k]
-        if step < 2 * len(order):
-            turn = min(step, 2 * len(order) - 1 - step)
-            cost = rows * width * 2e-6 / 2 ** (turn + 1) / rate
-            uses = {0: {"x": 1}, 1: {"end": 1}}.get(order[turn], {"end": 1, "mid": 2})
+        _, rows, depth, _, _ = chunks[k]
+        if step < bits + depth:
+            cost = trade_size(rows, depth, bits, step) * width * 2e-6 / rate
+            uses = {0: {"x": 1}, 1: {"end": 1}}.get(trade_bit(depth, bits, step), {"end": 1, "mid": 2})
             through = clock
             for link, share in uses.items():
                 free[link] = max(free.get(link, points[0]), clock) + share * cost
@@ -141,6 +156,8 @@
     dkt,
     dvt,
     ctx_s,
+    mixed_s,
+    gtok_s,
     vec,
     vec_in,
     sx,
@@ -245,13 +262,13 @@
     chunks = pieces(n, heads)
 
     def rows_of(k, first, size):
-        step = min(chunks[k][1] // n, 128)
+        step = min(chunks[k][1] // 2 ** chunks[k][2], 128)
         return pl.ds(pl.multiple_of(chunks[k][0] + first, step), size)
 
     def first_of(k, q):
         first = 0
         for p in range(q):
-            first = first + ((dp // 2 ** chunks[k][2][p]) % 2) * (chunks[k][1] // 2 ** (p + 1))
+            first = first + ((dp // 2**p) % 2) * (chunks[k][1] // 2 ** (p + 1))
         return first
 
     def kept(k, q):
@@ -259,41 +276,51 @@
 
     def given(k, q):
         size = chunks[k][1] // 2**q
-        bit = (dp // 2 ** chunks[k][2][q - 1]) % 2
+        bit = (dp // 2 ** (q - 1)) % 2
         return rows_of(k, first_of(k, q - 1) + (1 - bit) * size, size)
 
-    def landing(k, q):
-        first, rows, _ = chunks[k]
-        return pl.ds(first + rows - rows // 2 ** (q - 1), rows // 2**q)
+    def landing(k, step):
+        _, rows, depth, base, _ = chunks[k]
+        low = sum(trade_size(rows, depth, bits, p) for p in range(step))
+        return pl.ds(base + low, trade_size(rows, depth, bits, step))
 
     def ar_copy(k, step):
         sems = (ar_send.at[step, k], ar_recv.at[step, k])
-        order = chunks[k][2]
+        depth = chunks[k][2]
+        who = peers[trade_bit(depth, bits, step)]
         if step < bits:
-            return send(sx.at[landing(k, step + 1)], rx.at[landing(k, step + 1)], *sems, peers[order[step]])
-        q = 2 * bits - step
-        piece = res.at[kept(k, q)]
-        return send(piece, piece, *sems, peers[order[q - 1]])
+            return send(sx.at[landing(k, step)], rx.at[landing(k, step)], *sems, who)
+        piece = res.at[kept(k, depth - (step - bits))]
+        return send(piece, piece, *sems, who)
+
+    def chunk_out(k):
+        rows = kept(k, 0)
+        return pltpu.make_async_copy(res.at[rows], res_o.at[rows], out_sem.at[2 + k])
 
     def advance(k, step):
+        depth = chunks[k][2]
         if step > 0:
             ar_copy(k, step - 1).wait()
         if 1 <= step <= bits:
-            mine = kept(k, step)
-            done = acc[mine, :] + rx[landing(k, step), :].astype(F32)
+            mine = kept(k, min(step, depth))
+            had = acc[mine, :] if step <= depth else sx[landing(k, step - 1), :].astype(F32)
+            done = had + rx[landing(k, step - 1), :].astype(F32)
             if step < bits:
                 acc[mine, :] = done
             else:
                 res[mine, :] = done.astype(BF16)
         if step < bits:
-            sx[landing(k, step + 1), :] = acc[given(k, step + 1), :].astype(BF16)
-        if step < 2 * bits:
+            gone = given(k, step + 1) if step < depth else kept(k, depth)
+            sx[landing(k, step), :] = acc[gone, :].astype(BF16)
+        if step < bits + depth:
             ar_copy(k, step).start()
+        else:
+            chunk_out(k).start()
 
     first_it = 9
-    points = [-14.2, -12.3, -10.4, -8.9]
+    points = [-11.8, -9.9, -8.0]
     lead = len(points)
-    points += [-7.4 + FRONT * (u + 1) for u in range(heads * count)]
+    points += [-7.8 + FRONT * (u + 1) for u in range(heads * count)]
     mid = len(points)
     ends = []
     clock = 0.0
@@ -302,14 +329,14 @@
             for _ in range(i + 1):
                 clock += UNIT
                 points.append(clock)
-            clock += 0.7 if h < heads - 1 else 1.6
+            clock += 0.7
         ends.append(clock)
     last_time = clock
     ready = [points[0]] * 3 + [points[2]] * 3 + ends
     ready += [last_time] * (len(chunks) - len(ready))
     ticks = {}
     after = []
-    for when, u, k, step in plan(chunks, ready, points, width):
+    for when, u, k, step in plan(bits, chunks, ready, points, width):
         if u < len(points):
             ticks.setdefault(u, []).append(functools.partial(advance, k, step))
         else:
@@ -407,6 +434,12 @@
         mix = dot(ctx, wd[...], 0, 0) + x_s[mine, :].astype(F32)
         x_s[mine, :] = mix.astype(BF16)
 
+    def feed_part(rows):
+        part = dot(s_s[rows, :], we[...], 1, 1)
+        vec[2:3, :] += jnp.sum(part * n1_s[rows, :].astype(F32), 0, keepdims=True)
+        vec[3:4, :] += jnp.sum(part, 0, keepdims=True)
+        return part * gain2
+
     def phase(it, _):
         late = it // 7 > 0
         b = mate(jnp.where(late, 2 + (it + 1) % 2, it % 4))
@@ -438,7 +471,7 @@
 
             forward(b, slot, settle)
 
-        @pl.when(((it > 3) & (it < 7)) | (it == 13))
+        @pl.when(((it > 3) & (it < 7)) | (it == 11))
         def _():
             front(jnp.where(late, count - 1, it - 4))
 
@@ -461,23 +494,20 @@
         def _():
             slope = hold[4 + slot].astype(F32)
             grad_pre = (dot(g_s[rows, :], wc[...], 1, 1) * slope).astype(BF16)
-            hold[slot] = grad_pre
+            s_s[rows, :] = grad_pre
             vec[5:6, :] += jnp.sum(grad_pre.astype(F32), 0, keepdims=True)
             acc[width : 2 * width] += dot(hold[2 + slot], grad_pre, 0, 0)
-
-        @pl.when((it < 2) | (it == 11) | (it == 12))
-        def _():
-            part = dot(hold[slot], we[...], 1, 1)
-            s_s[rows, :] = (part * gain2).astype(BF16)
-            vec[2:3, :] += jnp.sum(part * hold[2 + slot].astype(F32), 0, keepdims=True)
-            vec[3:4, :] += jnp.sum(part, 0, keepdims=True)
             grad_ctx = dot(wd[...], g_s[rows, :], 1, 1).astype(BF16)
             for h in range(heads):
                 dot_s[h, :, rows] = grad_ctx[h * HD : (h + 1) * HD]
 
+        @pl.when(it < 2)
+        def _():
+            s_s[rows, :] = feed_part(rows).astype(BF16)
+
         return 0
 
-    lax.fori_loop(0, 14, phase, 0)
+    lax.fori_loop(0, 12, phase, 0)
     for k in (1, 2, 3, 5):
         gather[k].wait_send()
     pl.semaphore_signal(free_sem.at[0], inc=1, device_id=sib, device_id_type=MESH)
@@ -600,25 +630,22 @@
             grads = acc[pl.ds(pl.multiple_of(at, HD), 3 * HD), :]
             vec[0:1, :] += jnp.sum(w32 * grads, 0, keepdims=True)
 
-        @pl.when(h == heads - 1)
-        def _():
-            @pl.when(i < count - 1)
-            def _():
-                pass_on(i + 1, 1)
-
-            parts = [(qa[g, :HD, mine], kt[g, :, mine], va[g, :HD, mine]) for g in range(heads)]
-            every = jnp.concatenate([x for three in parts for x in three], 0)
-            part = dot(every, wt[...], 0, 0) * gain1 + s_s[mine, :].astype(F32)
-            s_s[mine, :] = part.astype(BF16)
-            hand_over(i, 1)
-            ones = jnp.ones((8, blk), BF16)
-            vec[6:7, : 3 * local] += dot(ones, every, 1, 1)[:1]
-
         return 0
 
     lax.fori_loop(0, heads * count, attend, 0)
+
+    def token_grads(r):
+        i = mate(r)
+        mine = block(i)
+        parts = [(qa[h, :HD, mine], kt[h, :, mine], va[h, :HD, mine]) for h in range(heads)]
+        every = jnp.concatenate([x for three in parts for x in three], 0)
+        fed = s_s[mine, :].astype(F32) if r < 2 else feed_part(mine)
+        s_s[mine, :] = (dot(every, wt[...], 0, 0) * gain1 + fed).astype(BF16)
+        hand_over(i, 1)
+        ones = jnp.ones((8, blk), BF16)
+        vec[6:7, : 3 * local] += dot(ones, every, 1, 1)[:1]
+
     again = pltpu.make_async_copy(tok, n1_s.at[own], in_sem.at[0])
-    again.start()
 
     swaps = peers + [sib, across]
     inside = len(peers)
@@ -641,10 +668,17 @@
         grad_bias = jnp.sum(w32 * column, 0, keepdims=True)
         vec[1:2, :] = grad_bias
         vec[0:1, :] = (vec[0:1, :] - bias1 * grad_bias) / gain1
-        vec[2:3, :] = (vec[2:3, :] - bias2 * vec[3:4, :]) / gain2
+        vec[2:3, :] = (vec[2:3, :] - bias1 * vec[3:4, :]) / gain1
         vec[4:5, :] = jnp.sum(g_s[own, :].astype(F32), 0, keepdims=True)
+        again.start()
+
+    out_copies = [
+        pltpu.make_async_copy(mixed_s, mixed_o, out_sem.at[0]),
+        pltpu.make_async_copy(gtok_s, gtok_o, out_sem.at[1]),
+    ]
 
     def tokens_out():
+        to_sib(t, 1).wait_recv()
         for w in range(2):
             to_owner(flip(t, 2), w).wait()
         again.wait()
@@ -655,15 +689,21 @@
         for w in (2 * chip_bit, 4):
             mix += hold[w].astype(F32)
             s += hold[w + 1].astype(F32)
-        mixed_o[...] = mix.astype(BF16)
+        mixed_s[...] = mix.astype(BF16)
         unit, inverse = unit_rows(rows)
-        gtok_o[...] = g_s[own, :].astype(F32) + inverse * (
+        gtok_s[...] = g_s[own, :].astype(F32) + inverse * (
             s - jnp.mean(s, -1, keepdims=True) - unit * jnp.mean(s * unit, -1, keepdims=True)
         )
+        for copy in out_copies:
+            copy.start()
 
     jobs = list(after)
-    jobs.append((last_time + 2.9, vectors))
-    jobs.append((last_time + 3.0, functools.partial(pass_on, 0, 1)))
+    jobs.append((last_time + 1.7, functools.partial(token_grads, 3)))
+    jobs.append((last_time + 3.7, functools.partial(token_grads, 2)))
+    jobs.append((last_time + 5.7, functools.partial(token_grads, 1)))
+    jobs.append((last_time + 6.8, lambda: pass_on(mate(2), 1)))
+    jobs.append((last_time + 7.3, functools.partial(token_grads, 0)))
+    jobs.append((last_time + 8.5, vectors))
     for q in range(len(swaps)):
 
         def trade(q=q):
@@ -671,13 +711,11 @@
                 finish_swap(q - 1)
             swap(q).start()
 
-        jobs.append((last_time + 4.0 + 3.5 * q, trade))
-    jobs.append((last_time + 4.0 + 3.5 * len(swaps), lambda: finish_swap(len(swaps) - 1)))
-    jobs.append((last_time + 20.0, tokens_out))
+        jobs.append((last_time + 9.5 + 3.2 * q, trade))
+    jobs.append((last_time + 9.5 + 3.2 * len(swaps), lambda: finish_swap(len(swaps) - 1)))
+    jobs.append((last_time + 27.0, tokens_out))
     for _, job in sorted(jobs, key=lambda pair: pair[0]):
         job()
-    out_copy = pltpu.make_async_copy(res, res_o, out_sem.at[0])
-    out_copy.start()
     vec_o[...] = vec[...]
     for i in range(count):
 
@@ -686,39 +724,73 @@
             for w in range(2):
                 to_sib(i, w).wait_send()
 
-    out_copy.wait()
-
-
-def finish(res, mixed, gtok, vec, *outs):
-    (mixed_o, gtok_o, gain1_o, bias1_o, gain2_o, bias2_o, qkv_o, qkvb_o, wd_o, db_o, we_o, be_o, wc_o, cb_o) = outs
-    step = pl.program_id(0)
+    for copy in out_copies:
+        copy.wait()
+    for k in range(len(chunks)):
+        chunk_out(k).wait()
+
+
+def finish(res, mixed, gtok, vec, *refs):
+    outs, (low, high, mid_m, mid_g, moved, in_sem, out_sem) = refs[:14], refs[14:]
+    mixed_o, gtok_o, gain1_o, bias1_o, gain2_o, bias2_o, qkv_o, qkvb_o, wd_o, db_o, we_o, be_o, wc_o, cb_o = outs
     width = res.shape[1]
     heads = wd_o.shape[0] // HD
-    band = 4 * HD
-
-    @pl.when(step == 0)
-    def _():
-        wc_o[...] = res[...].astype(F32)
-        mixed_o[...] = mixed[...]
-        gtok_o[...] = gtok[...]
-        for ref, row in ((gain1_o, 0), (bias1_o, 1), (gain2_o, 2), (bias2_o, 3), (db_o, 4), (cb_o, 4), (be_o, 5)):
-            ref[...] = vec[row, :]
-        for h in range(heads):
-            for c in range(3):
-                lo = (3 * h + c) * HD
-                qkvb_o[c : c + 1, h * HD : (h + 1) * HD] = vec[6:7, lo : lo + HD]
-
-    @pl.when(step == 1)
-    def _():
-        we_o[...] = res[...].astype(F32)
-
-    @pl.when(step == 2)
-    def _():
-        for h in range(heads):
-            lo = h * band
-            for c in range(3):
-                qkv_o[c, h * HD : (h + 1) * HD, :] = res[lo + c * HD : lo + (c + 1) * HD, :].astype(F32)
-            wd_o[h * HD : (h + 1) * HD, :] = res[lo + 3 * HD : lo + band, :].astype(F32)
+    count = low.shape[0] // SUB
+    passing = [
+        pltpu.make_async_copy(mixed, mid_m, moved.at[0]),
+        pltpu.make_async_copy(gtok, mid_g, moved.at[1]),
+    ]
+    leaving = [
+        pltpu.make_async_copy(mid_m, mixed_o, moved.at[2]),
+        pltpu.make_async_copy(mid_g, gtok_o, moved.at[3]),
+    ]
+
+    def rows(k):
+        return pl.ds(k * SUB, SUB)
+
+    comes = [pltpu.make_async_copy(res.at[rows(k)], low.at[rows(k)], in_sem.at[k]) for k in range(count)]
+    goes = []
+    for k in range(6):
+        where = (wc_o, we_o)[k // 3].at[rows(k % 3)]
+        goes.append([pltpu.make_async_copy(high.at[rows(k)], where, out_sem.at[k])])
+    for h in range(heads):
+        first = (6 + h) * SUB
+        places = [qkv_o.at[c, h * HD : (h + 1) * HD, :] for c in range(3)] + [wd_o.at[h * HD : (h + 1) * HD]]
+        goes.append(
+            [
+                pltpu.make_async_copy(
+                    high.at[pl.ds(first + c * HD, HD)], place, out_sem.at[6 + 4 * h + c]
+                )
+                for c, place in enumerate(places)
+            ]
+        )
+    for copy in passing + comes:
+        copy.start()
+    for ref, row in (
+        (gain1_o, 0),
+        (bias1_o, 1),
+        (gain2_o, 2),
+        (bias2_o, 3),
+        (db_o, 4),
+        (cb_o, 4),
+        (be_o, 5),
+    ):
+        ref[...] = vec[row, :]
+    for h in range(heads):
+        for c in range(3):
+            lo = (3 * h + c) * HD
+            qkvb_o[c : c + 1, h * HD : (h + 1) * HD] = vec[6:7, lo : lo + HD]
+    for k in range(count):
+        comes[k].wait()
+        high[rows(k), :] = low[rows(k), :].astype(F32)
+        for copy in goes[k]:
+            copy.start()
+        if k == 0:
+            for come, go in zip(passing, leaving):
+                come.wait()
+                go.start()
+    for copy in [x for some in goes for x in some] + leaving:
+        copy.wait()
 
 
 def shards(
@@ -747,6 +819,7 @@
     bits = n.bit_length() - 1
     swaps = bits + 2
     parts = len(pieces(n, heads))
+    room = sum(chunk[4] for chunk in pieces(n, heads))
     cosine, sine = angle_rows(total)
     vmem = pl.BlockSpec(memory_space=pltpu.VMEM)
     smem = pl.BlockSpec(memory_space=pltpu.SMEM)
@@ -762,7 +835,7 @@
             jax.ShapeDtypeStruct((8, width), F32),
         ),
         in_specs=[hbm, hbm, smem] + [vmem] * 7 + [hbm, vmem, hbm, hbm, hbm, vmem, vmem],
-        out_specs=[vmem, vmem, hbm, vmem],
+        out_specs=[hbm, hbm, hbm, vmem],
         scratch_shapes=[
             pltpu.VMEM((total, width), BF16),
             pltpu.VMEM((total, width), BF16),
@@ -786,10 +859,12 @@
             pltpu.VMEM((HD, total), F32),
             pltpu.VMEM((HD, total), F32),
             pltpu.VMEM((heads, HD, total), BF16),
+            pltpu.VMEM((blk, width), BF16),
+            pltpu.VMEM((blk, width), F32),
             pltpu.VMEM((8, width), F32),
             pltpu.VMEM((swaps, 8, width), F32),
-            pltpu.VMEM((3 * width, width), BF16),
-            pltpu.VMEM((3 * width, width), BF16),
+            pltpu.VMEM((room, width), BF16),
+            pltpu.VMEM((room, width), BF16),
             dma((5 + 3 * heads,)),
             dma((6,)),
             dma((6,)),
@@ -799,7 +874,7 @@
             dma((2 * bits, parts)),
             dma((swaps,)),
             dma((swaps,)),
-            dma((1,)),
+            dma((2 + parts,)),
             pltpu.SemaphoreType.REGULAR((2,)),
         ],
         compiler_params=pltpu.CompilerParams(
@@ -825,31 +900,20 @@
         sine,
     )
 
-    def whole(*shape):
-        return pl.BlockSpec(shape, lambda g: (0,) * len(shape))
-
     vector = jax.ShapeDtypeStruct((width,), F32)
     outs = pl.pallas_call(
         finish,
         name="finish",
-        grid=(3,),
-        in_specs=[
-            pl.BlockSpec((width, width), lambda g: (g, 0)),
-            whole(blk, width),
-            whole(blk, width),
-            whole(8, width),
-        ],
-        out_specs=[whole(blk, width), whole(blk, width)]
-        + [whole(width)] * 4
-        + [
-            whole(3, local, width),
-            whole(3, local),
-            whole(local, width),
-            whole(width),
-            whole(width, hidden),
-            whole(hidden),
-            whole(hidden, width),
-            whole(width),
+        in_specs=[hbm, hbm, hbm, vmem],
+        out_specs=[hbm, hbm] + [vmem] * 4 + [hbm, vmem, hbm, vmem, hbm, vmem, hbm, vmem],
+        scratch_shapes=[
+            pltpu.VMEM((3 * width, width), BF16),
+            pltpu.VMEM((3 * width, width), F32),
+            pltpu.VMEM((blk, width), BF16),
+            pltpu.VMEM((blk, width), F32),
+            dma((4,)),
+            dma((9,)),
+            dma((6 + 4 * heads,)),
         ],
         out_shape=(
             jax.ShapeDtypeStruct((blk, width), BF16),

time: 150 us -> 145 us (0.967)
  Pallas kernels: 149 us -> 144 us
    pallas_call x1, Pallas kernels: 141 us -> 136 us  [shards(): pl.pallas_call(functools.partial(core, n), name='core', out_shape=(jax.Sh...]
where the time goes in v5:
time: 145 us
  Pallas kernels  144 us (99%)
  between operations  1.47 us (1%)
    pallas_call x1, Pallas kernels, shards(): pl.pallas_call(functools.partial(core, n), name='core', out_shape=(jax.Sh...  136 us
    pallas_call x1, Pallas kernels, shards(): pl.pallas_call(finish, name='finish', in_specs=[hbm, hbm, hbm, vmem], out...  7.62 us

profile of v5, /device:TPU:0, one launch (start us, length us, event | category | flops | bytes accessed | tf_op | source)
XLA Modules:
  0.0 145.1 jit_solution(16798993679218781692)
XLA Ops:
  1.3 136.0 %core.1 = (bf16[512,768]{1,0:T(8,128)(2,1)}, f32[512,768]{1,0:T(8,128)}, bf16[2304,768]{1,0:T(8,128)(2,1)}, f32[8,768]{1,0:T(8,128)}) custom-call(bf16[512,768]{1,0:T(8,128)(2,1)} %tok.1, bf16[512,768]{1,0:T(8,128)(2,1)} %cot.1, s32[1]{0:T(128)S(6)} %copy.31.len_ref, f32[768]{0:T(1024)} %gain1_r.1, f32[768]{0:T(1024)} %bias1_r.1, f32[768]{0:T(1024)} %gain2_r.1, ...), custom_call_target="tpu_custom_call" | custom-call | tf_op jit(solution)/shard_map/core/pallas_call | solution.py:828
  137.3 7.6 %finish.1 = (bf16[512,768]{1,0:T(8,128)(2,1)}, f32[512,768]{1,0:T(8,128)}, f32[768]{0:T(1024)}, f32[768]{0:T(1024)}, f32[768]{0:T(1024)}, /*index=5*/f32[768]{0:...) custom-call(bf16[2304,768]{1,0:T(8,128)(2,1)} %get-tuple-element.32., ...), custom_call_target="tpu_custom_call" | custom-call | tf_op jit(solution)/shard_map/finish/pallas_call | solution.py:904

commit v6 on v5

--- a/solution.py
+++ b/solution.py
@@ -81,7 +81,7 @@
     return step if step < bits else depth - (step - bits) - 1
 
 
-def plan(bits, chunks, ready, points, width, margin=0.5, rate=0.045, delay=3.0, work=0.2):
+def plan(bits, chunks, ready, points, width, margin=0.3, rate=0.043, delay=2.2, work=0.2):
     free = {}
     clock = points[0]
     reached = 0

time: 145 us -> 142 us (0.979)
  Pallas kernels: 144 us -> 140 us
    pallas_call x1, Pallas kernels: 136 us -> 133 us  [shards(): pl.pallas_call(functools.partial(core, n), name='core', out_shape=(jax.Sh...]
where the time goes in v6:
time: 142 us
  Pallas kernels  140 us (99%)
  between operations  1.47 us (1%)
    pallas_call x1, Pallas kernels, shards(): pl.pallas_call(functools.partial(core, n), name='core', out_shape=(jax.Sh...  133 us
    pallas_call x1, Pallas kernels, shards(): pl.pallas_call(finish, name='finish', in_specs=[hbm, hbm, hbm, vmem], out...  7.62 us

profile of v6, /device:TPU:0, one launch (start us, length us, event | category | flops | bytes accessed | tf_op | source)
XLA Modules:
  0.0 141.9 jit_solution(17910960656090993517)
XLA Ops:
  1.3 132.8 %core.1 = (bf16[512,768]{1,0:T(8,128)(2,1)}, f32[512,768]{1,0:T(8,128)}, bf16[2304,768]{1,0:T(8,128)(2,1)}, f32[8,768]{1,0:T(8,128)}) custom-call(bf16[512,768]{1,0:T(8,128)(2,1)} %tok.1, bf16[512,768]{1,0:T(8,128)(2,1)} %cot.1, s32[1]{0:T(128)S(6)} %copy.31.len_ref, f32[768]{0:T(1024)} %gain1_r.1, f32[768]{0:T(1024)} %bias1_r.1, f32[768]{0:T(1024)} %gain2_r.1, ...), custom_call_target="tpu_custom_call" | custom-call | tf_op jit(solution)/shard_map/core/pallas_call | solution.py:828
  134.1 7.6 %finish.1 = (bf16[512,768]{1,0:T(8,128)(2,1)}, f32[512,768]{1,0:T(8,128)}, f32[768]{0:T(1024)}, f32[768]{0:T(1024)}, f32[768]{0:T(1024)}, /*index=5*/f32[768]{0:...) custom-call(bf16[2304,768]{1,0:T(8,128)(2,1)} %get-tuple-element.32., ...), custom_call_target="tpu_custom_call" | custom-call | tf_op jit(solution)/shard_map/finish/pallas_call | solution.py:904

commit v7 on v6

--- a/solution.py
+++ b/solution.py
@@ -59,7 +59,7 @@
     base = 0
     for k in range(count):
         last = k == count - 1
-        parts = 2 if last and n <= 16 else 1
+        parts = 4 if last and n <= 16 else 1
         size = SUB // parts
         depth = max(bits - 2, 1) if last else bits - 1
         room = size - size // 2**depth + (bits - depth) * (size // 2**depth)
@@ -567,8 +567,8 @@
 
         lax.fori_loop(0, count, one, 0)
 
-    ticks.setdefault(mid + 3, []).insert(0, mixes_over)
-    ticks.setdefault(mid + 7, []).insert(0, mixes_on)
+    ticks.setdefault(mid + 6, []).insert(0, mixes_over)
+    ticks.setdefault(mid + 13, []).insert(0, mixes_on)
 
     def attend(visit, _):
         h = visit // count
@@ -713,7 +713,7 @@
 
         jobs.append((last_time + 9.5 + 3.2 * q, trade))
     jobs.append((last_time + 9.5 + 3.2 * len(swaps), lambda: finish_swap(len(swaps) - 1)))
-    jobs.append((last_time + 27.0, tokens_out))
+    jobs.append((last_time + 31.0, tokens_out))
     for _, job in sorted(jobs, key=lambda pair: pair[0]):
         job()
     vec_o[...] = vec[...]

time: 142 us -> 142 us (level)
  no operation moved by 1% of the time
where the time goes in v7:
time: 142 us
  Pallas kernels  140 us (99%)
  between operations  1.47 us (1%)
    pallas_call x1, Pallas kernels, shards(): pl.pallas_call(functools.partial(core, n), name='core', out_shape=(jax.Sh...  132 us
    pallas_call x1, Pallas kernels, shards(): pl.pallas_call(finish, name='finish', in_specs=[hbm, hbm, hbm, vmem], out...  7.62 us

profile of v7, /device:TPU:0, one launch (start us, length us, event | category | flops | bytes accessed | tf_op | source)
XLA Modules:
  0.0 141.5 jit_solution(7883640188706437206)
XLA Ops:
  1.3 132.4 %core.1 = (bf16[512,768]{1,0:T(8,128)(2,1)}, f32[512,768]{1,0:T(8,128)}, bf16[2304,768]{1,0:T(8,128)(2,1)}, f32[8,768]{1,0:T(8,128)}) custom-call(bf16[512,768]{1,0:T(8,128)(2,1)} %tok.1, bf16[512,768]{1,0:T(8,128)(2,1)} %cot.1, s32[1]{0:T(128)S(6)} %copy.31.len_ref, f32[768]{0:T(1024)} %gain1_r.1, f32[768]{0:T(1024)} %bias1_r.1, f32[768]{0:T(1024)} %gain2_r.1, ...), custom_call_target="tpu_custom_call" | custom-call | tf_op jit(solution)/shard_map/core/pallas_call | solution.py:828
  133.7 7.6 %finish.1 = (bf16[512,768]{1,0:T(8,128)(2,1)}, f32[512,768]{1,0:T(8,128)}, f32[768]{0:T(1024)}, f32[768]{0:T(1024)}, f32[768]{0:T(1024)}, /*index=5*/f32[768]{0:...) custom-call(bf16[2304,768]{1,0:T(8,128)(2,1)} %get-tuple-element.32., ...), custom_call_target="tpu_custom_call" | custom-call | tf_op jit(solution)/shard_map/finish/pallas_call | solution.py:904
